TPU v7x, 32 devices: a whole 2x2x4 slice. The times are simulated.
32 devices in a mesh: groups: 2 (over y), sample: 4 (over z), fsdp: 2 (over x), prompt: 2 (over core).
Axes of the slice: x: 2, y: 2, z: 4, core: 2. Of those that a mesh axis runs over, the one named last changes fastest.
Arguments:
- queries: bfloat16 [4, 4, 256, 4096], P(('groups', 'prompt'), 'sample', 'fsdp'), parts along dimension 0, may hold values from -16 to 16
- completion_keys: bfloat16 [4, 4, 256, 512], P(('groups', 'prompt'), 'sample', 'fsdp'), parts along dimension 0, may hold values from -6 to 6
- completion_values: bfloat16 [4, 4, 256, 512], P(('groups', 'prompt'), 'sample', 'fsdp'), parts along dimension 0, may hold values from -6 to 6
- prompt_keys: bfloat16 [4, 8, 512], P(('groups', 'prompt'), ('sample', 'fsdp')), parts along dimension 0, may hold values from -6 to 6
- prompt_values: bfloat16 [4, 8, 512], P(('groups', 'prompt'), ('sample', 'fsdp')), parts along dimension 0, may hold values from -6 to 6
- output_grad: bfloat16 [4, 4, 256, 4096], P(('groups', 'prompt'), 'sample', 'fsdp'), parts along dimension 0, may hold values from -6 to 6
- lengths: int32 [4, 4], P(('groups', 'prompt'), 'sample'), parts along dimension 0, may hold values from 64 to 256
Outputs:
- attention_out: bfloat16 [4, 4, 256, 4096], P(('groups', 'prompt'), 'sample', 'fsdp'), parts along dimension 0
- query_grad: bfloat16 [4, 4, 256, 4096], P(('groups', 'prompt'), 'sample', 'fsdp'), parts along dimension 0
- completion_key_grad: float32 [4, 4, 256, 512], P(('groups', 'prompt'), 'sample', 'fsdp'), parts along dimension 0
- completion_value_grad: float32 [4, 4, 256, 512], P(('groups', 'prompt'), 'sample', 'fsdp'), parts along dimension 0
- shared_prompt_key_gradient: float32 [4, 8, 512], P(('groups', 'prompt'), ('sample', 'fsdp')), parts along dimension 0
- shared_prompt_value_gradient: float32 [4, 8, 512], P(('groups', 'prompt'), ('sample', 'fsdp')), parts along dimension 0
There are 2 independent parts, one for each index of `groups`. A program takes and returns all parts, laid end to end along the dimension named above; each array names one. Nothing has to cross between parts.
All inputs are finite; a program needn't handle non-finite values.
Results may differ from a plain program's by a relative error of at most 0.02.
Values may be sent and summed in bfloat16 or wider, within the bound.
No kernel may reach another device: no remote copies, remote signals or barrier semaphores. Data moves between devices by JAX's collectives and lax.ppermute only.
A program may use at most 128 MiB of HBM per device.

v0:
```python
import functools

import jax
import jax.numpy as jnp
from jax import lax
from jax.experimental import pallas as pl
from jax.experimental.pallas import tpu as pltpu
from jax.sharding import PartitionSpec as P

HEAD_DIM = 128
LOG2E = 1.4426950408889634
UNITS = 2
PARTS = 4
VMEM_LIMIT = 24 << 20

NT = (((1,), (1,)), ((), ()))
NN = (((1,), (0,)), ((), ()))


def mm(a, b, dims=NN):
    return lax.dot_general(a, b, dims, preferred_element_type=jnp.float32)


def pad_rows(x, rows):
    if x.shape[0] == rows:
        return x
    return jnp.concatenate([x, jnp.zeros((rows - x.shape[0], x.shape[1]), x.dtype)], 0)


def attend_kernel(shifts, share, q_ref, g_ref, k_ref, v_ref, *refs):
    earlier = refs[: 2 * shifts]
    prefix, out, dq, dk, dv = refs[2 * shifts : 2 * shifts + 5]
    rest = refs[2 * shifts + 5 :]
    dback = rest[0] if shifts else None
    dprefix = rest[-1]
    rows = q_ref.shape[0]
    prompt = prefix.shape[0]
    padded = -(-prompt // 16) * 16
    before = padded + shifts * rows
    chunk = min(rows, 256 // share)
    steps = rows // chunk
    place = lax.axis_index("fsdp")
    scale = HEAD_DIM ** -0.5
    factor = scale * LOG2E
    neg = jnp.float32(-jnp.inf)

    units = k_ref.shape[1] // HEAD_DIM
    sides = []
    for u in range(units):
        col = slice(u * HEAD_DIM, (u + 1) * HEAD_DIM)
        lead_k = pad_rows(prefix[:, 0, col], padded).astype(jnp.bfloat16)
        lead_v = pad_rows(prefix[:, 1, col], padded).astype(jnp.bfloat16)
        keys = jnp.concatenate(
            [lead_k] + [earlier[2 * s][:, col] for s in range(shifts)] + [k_ref[:, col]], 0
        )
        values = jnp.concatenate(
            [lead_v] + [earlier[2 * s + 1][:, col] for s in range(shifts)] + [v_ref[:, col]], 0
        )
        sides.append((keys, values, keys.T, values.T))
    bias = [jnp.where(place >= s + 1, jnp.float32(0.0), neg) for s in range(shifts)]
    causal = lax.broadcasted_iota(jnp.int32, (chunk, share * chunk), 0) <= lax.rem(
        lax.broadcasted_iota(jnp.int32, (chunk, share * chunk), 1), chunk
    )
    heads = [
        [slice((u * share + h) * HEAD_DIM, (u * share + h + 1) * HEAD_DIM) for h in range(share)]
        for u in range(units)
    ]

    def first(u, i):
        keys, values = sides[u][:2]
        head = heads[u]
        part = slice(i * chunk, (i + 1) * chunk)
        q = jnp.concatenate([q_ref[part, c] for c in head], 0)
        g = jnp.concatenate([g_ref[part, c] for c in head], 0)
        seen = before + (i + 1) * chunk
        return q, g, mm(keys[:seen], q, NT), mm(values[:seen], g, NT)

    def second(i, scores, dprob):
        seen = before + (i + 1) * chunk
        lead = scores[:prompt]
        back = [scores[padded + s * rows : padded + (s + 1) * rows] for s in range(shifts)]
        full = scores[before : seen - chunk]
        last = jnp.where(causal, scores[seen - chunk :], neg)
        top = jnp.maximum(jnp.max(last, 0, keepdims=True), jnp.max(lead, 0, keepdims=True))
        if i:
            top = jnp.maximum(top, jnp.max(full, 0, keepdims=True))
        for s in range(shifts):
            top = jnp.maximum(top, jnp.max(back[s], 0, keepdims=True) + bias[s])
        top = top * factor
        parts = [jnp.exp2(lead * factor - top)]
        if padded != prompt:
            parts.append(jnp.zeros((padded - prompt, lead.shape[1]), jnp.float32))
        parts += [jnp.exp2(back[s] * factor - (top - bias[s])) for s in range(shifts)]
        if i:
            parts.append(jnp.exp2(full * factor - top))
        parts.append(jnp.exp2(last * factor - top))
        expo = jnp.concatenate(parts, 0)
        inverse = 1.0 / jnp.sum(expo, 0, keepdims=True)
        dot = jnp.sum(expo * dprob, 0, keepdims=True) * inverse
        probs = expo * inverse
        sgrad = (probs * (dprob - dot)).astype(jnp.bfloat16)
        return probs.astype(jnp.bfloat16), sgrad

    def deep(left, right):
        total = None
        for at in range(0, right.shape[0], 256):
            end = min(at + 256, right.shape[0])
            term = mm(left[:, at:end], right[at:end])
            total = term if total is None else total + term
        return total

    def third(u, i, q, g, probs, sgrad, acc):
        keys_t, values_t = sides[u][2:]
        head = heads[u]
        seen = before + (i + 1) * chunk
        part = slice(i * chunk, (i + 1) * chunk)
        mixed = deep(values_t[:, :seen], probs).astype(jnp.bfloat16).T
        dquery = (deep(keys_t[:, :seen], sgrad) * scale).astype(jnp.bfloat16).T
        for h, c in enumerate(head):
            out[part, c] = mixed[h * chunk : (h + 1) * chunk]
            dq[part, c] = dquery[h * chunk : (h + 1) * chunk]
        new = mm(sgrad, q), mm(probs, g)
        if acc is None:
            return new
        old = acc[0].shape[0]
        return tuple(jnp.concatenate([a + n[:old], n[old:]], 0) for a, n in zip(acc, new))

    def finish(u, acc):
        col = slice(u * HEAD_DIM, (u + 1) * HEAD_DIM)
        key_term, value_term = acc[0] * scale, acc[1]
        dk[:, col] = key_term[before:]
        dv[:, col] = value_term[before:]
        for s in range(shifts):
            at = slice(padded + s * rows, padded + (s + 1) * rows)
            dback[s, 0, :, col] = key_term[at].astype(jnp.bfloat16)
            dback[s, 1, :, col] = value_term[at].astype(jnp.bfloat16)
        dprefix[:, 0, col] = key_term[:prompt]
        dprefix[:, 1, col] = value_term[:prompt]

    order = [(u, i) for u in range(units) for i in range(steps)]
    acc = [None] * units

    def close(work):
        u, i = work[:2]
        acc[u] = third(*work, acc[u])
        if i == steps - 1:
            finish(u, acc[u])

    ahead, behind = first(*order[0]), None
    for n, (u, i) in enumerate(order):
        q, g, scores, dprob = ahead
        if n + 1 < len(order):
            ahead = first(*order[n + 1])
        if behind is not None:
            close(behind)
        probs, sgrad = second(i, scores, dprob)
        behind = (u, i, q, g, probs, sgrad)
    close(behind)


def attend(queries, grads, keys, values, earlier, prefix):
    rows, width = queries.shape
    groups = keys.shape[1] // HEAD_DIM
    share = width // HEAD_DIM // groups
    units = UNITS if groups % UNITS == 0 else 1
    shifts = len(earlier) // 2
    prompt = prefix.shape[0]
    wide = pl.BlockSpec((rows, units * share * HEAD_DIM), lambda i: (0, i))
    narrow = pl.BlockSpec((rows, units * HEAD_DIM), lambda i: (0, i))
    lead = pl.BlockSpec((prompt, 2, units * HEAD_DIM), lambda i: (0, 0, i))
    outs = [
        jax.ShapeDtypeStruct((rows, width), jnp.bfloat16),
        jax.ShapeDtypeStruct((rows, width), jnp.bfloat16),
        jax.ShapeDtypeStruct(keys.shape, jnp.float32),
        jax.ShapeDtypeStruct(keys.shape, jnp.float32),
    ]
    out_specs = [wide, wide, narrow, narrow]
    if shifts:
        outs.append(jax.ShapeDtypeStruct((shifts, 2) + keys.shape, jnp.bfloat16))
        out_specs.append(pl.BlockSpec((shifts, 2, rows, units * HEAD_DIM), lambda i: (0, 0, 0, i)))
    outs.append(jax.ShapeDtypeStruct(prefix.shape, jnp.float32))
    out_specs.append(lead)
    result = pl.pallas_call(
        functools.partial(attend_kernel, shifts, share),
        out_shape=outs,
        grid=(groups // units,),
        in_specs=[wide, wide, narrow, narrow] + [narrow] * (2 * shifts) + [lead],
        out_specs=out_specs,
        compiler_params=pltpu.CompilerParams(
            dimension_semantics=("arbitrary",), vmem_limit_bytes=VMEM_LIMIT
        ),
    )(queries, grads, keys, values, *earlier, prefix)
    if shifts:
        return result
    return list(result[:4]) + [None, result[4]]


def prepare_kernel(comp_span, length_ref, g_ref, *refs):
    sources, g_out, targets, sems = refs[:3], refs[3], refs[4:7], refs[7]
    copies = [pltpu.make_async_copy(a, b, sems.at[n]) for n, (a, b) in enumerate(zip(sources, targets))]

    @pl.when(pl.program_id(0) == 0)
    def _():
        for copy in copies:
            copy.start()

    rows, width = g_ref.shape
    length = length_ref[0, 0]
    ratio = jnp.float32(comp_span) / length.astype(jnp.float32)
    token = lax.axis_index("fsdp") * rows + lax.broadcasted_iota(jnp.int32, (rows, HEAD_DIM), 0)
    weight = jnp.where(token < length, ratio, jnp.float32(0.0))
    for at in range(0, width, HEAD_DIM):
        c = slice(at, at + HEAD_DIM)
        g_out[:, c] = (g_ref[:, c].astype(jnp.float32) * weight).astype(jnp.bfloat16)

    @pl.when(pl.program_id(0) == pl.num_programs(0) - 1)
    def _():
        for copy in copies:
            copy.wait()


def prepare(lengths, queries, grads, keys, values, comp_span):
    rows, width = grads.shape
    parts = PARTS if width % (PARTS * HEAD_DIM) == 0 else 1
    wide = pl.BlockSpec((rows, width // parts), lambda i: (0, i))
    whole = pl.BlockSpec(memory_space=pl.ANY)
    arrays = [pltpu.with_memory_space_constraint(x, pltpu.HBM) for x in (grads, queries, keys, values)]
    moved = 2 * 2 * (queries.size + grads.size + keys.size + values.size)
    g, q, k, v = pl.pallas_call(
        functools.partial(prepare_kernel, comp_span),
        out_shape=[jax.ShapeDtypeStruct(x.shape, x.dtype) for x in arrays],
        grid=(parts,),
        in_specs=[pl.BlockSpec(memory_space=pltpu.SMEM), wide, whole, whole, whole],
        out_specs=[wide, whole, whole, whole],
        scratch_shapes=[pltpu.SemaphoreType.DMA((3,))],
        cost_estimate=pl.CostEstimate(flops=grads.size, bytes_accessed=moved, transcendentals=0),
        compiler_params=pltpu.CompilerParams(
            dimension_semantics=("arbitrary",), vmem_limit_bytes=VMEM_LIMIT
        ),
    )(lengths, *arrays)
    return q, g, k, v


def shards(
    queries, completion_keys, completion_values, prompt_keys, prompt_values, output_grad, lengths
):
    fsdp = lax.axis_size("fsdp")
    everyone = fsdp * lax.axis_size("sample")
    rows = queries.shape[2]
    keys, values = completion_keys[0, 0], completion_values[0, 0]
    earlier = []
    for s in range(1, fsdp):
        ring = [(i, (i + s) % fsdp) for i in range(fsdp)]
        earlier += [lax.ppermute(keys, "fsdp", ring), lax.ppermute(values, "fsdp", ring)]
    line = jnp.stack([prompt_keys[0], prompt_values[0]], 1).astype(jnp.float32)
    prefix = lax.all_to_all(
        jnp.tile(line, (everyone, 1, 1)),
        ("sample", "fsdp"),
        split_axis=0,
        concat_axis=0,
        tiled=True,
    )
    q, g, k, v = prepare(lengths, queries[0, 0], output_grad[0, 0], keys, values, rows * fsdp)
    out, dq, dk, dv, dback, dprefix = attend(q, g, k, v, earlier, prefix)
    landed = []
    for s in range(1, fsdp):
        ring = [(i, (i - s) % fsdp) for i in range(fsdp)]
        landed.append(lax.ppermute(dback[s - 1], "fsdp", ring))
    shares = lax.all_to_all(dprefix, ("sample", "fsdp"), split_axis=0, concat_axis=0, tiled=True)
    for block in landed:
        block = block.astype(jnp.float32)
        dk, dv = dk + block[0], dv + block[1]
    total = jnp.sum(shares.reshape((everyone, -1) + shares.shape[1:]), 0)
    return (
        out[None, None],
        dq[None, None],
        dk[None, None],
        dv[None, None],
        total[None, :, 0],
        total[None, :, 1],
    )


def solution(mesh):
    wide = P(("groups", "prompt"), "sample", "fsdp", None)
    lead = P(("groups", "prompt"), ("sample", "fsdp"), None)
    in_specs = (wide, wide, wide, lead, lead, wide, P(("groups", "prompt"), "sample"))
    out_specs = (wide, wide, wide, wide, lead, lead)
    return jax.shard_map(shards, mesh=mesh, in_specs=in_specs, out_specs=out_specs, check_vma=False)
```

profile of v0, /device:TPU:0, one launch (start us, length us, event | category | flops | bytes accessed | tf_op | source)
XLA Modules:
  0.0 33.8 jit_solution(12420662393779387614)
XLA Ops:
  0.6 3.0 %collective-permute-start = (bf16[128,512]{1,0:T(8,128)(2,1)}, bf16[128,512]{1,0:T(8,128)(2,1)S(1)}, u32[]{:S(2)}, u32[]{:S(2)}) collective-permute-start(bf16[128,512]{1,0:T(8,128)(2,1)} %bitcast.29), channel_id=1, source_target_pairs={{0,2},{2,0},{1,3},{3,1},{4,6},{6,4},{5,7},{7,5},{8,10},{10,8},{9,1... | collective-permute-start | bytes 393224 | tf_op jit(solution)/shard_map/ppermute | solution.py:254
  3.7 0.0 copy-start.1
  3.7 0.0 copy-start
  3.7 0.1 collective-permute-start.1
  3.8 0.6 %copy-done.1 = bf16[1,1,512]{2,1,0:T(2,128)(2,1)S(1)} copy-done((bf16[1,1,512]{2,1,0:T(2,128)(2,1)S(1)}, bf16[1,1,512]{2,1,0:T(2,128)(2,1)}, u32[]{:S(2)}) %copy-start.1) | copy-done | bytes 1048
  4.3 0.0 copy-done
  4.4 0.6 %tile.2 = f32[8,2,512]{2,1,0:T(2,128)} broadcast(f32[2,512]{1,0:T(2,128)S(1)} %maximum_convert_fusion), dimensions={1,2} | broadcast | bytes 36864 | tf_op jit(solution)/shard_map/tile | solution.py:257
  5.0 5.7 %all-to-all-start = ((f32[8,2,512]{2,1,0:T(2,128)}), f32[8,2,512]{2,1,0:T(2,128)S(1)}, u32[]{:S(2)}, u32[]{:S(2)}) async-start(f32[8,2,512]{2,1,0:T(2,128)} %tile.2), calls=%async_computation | async-start | bytes 65536 | tf_op jit(solution)/shard_map/all_to_all | solution.py:256
  11.3 2.7 %shard_map.118 = (bf16[128,4096]{1,0:T(8,128)(2,1)S(1)}, bf16[128,4096]{1,0:T(8,128)(2,1)S(1)}, bf16[128,512]{1,0:T(8,128)(2,1)S(1)}, bf16[128,512]{1,0:T(8,128)(2,1)S(1)}) custom-call(s32[1,1]{1,0:T(1,128)S(6)} %copy.13.length_ref, bf16[128,4096]{1,0:T(8,128)(2,1)} %bitcast.27, bf16[128,4096]{1,0:T(8,128)(2,1)} %bitcast.28, bf16[128,512]{1,0:T(8,128)(2,1)} %bitcast.30, ...), custom_call_target="tpu_custom_call" | custom-call | flops 524288 | bytes 4718592 | tf_op jit(solution)/shard_map/pallas_call | solution.py:229
  14.0 3.4 %all-to-all-done.refs_2_ = f32[8,2,512]{2,1,0:T(2,128)S(1)} async-done(((f32[8,2,512]{2,1,0:T(2,128)}), f32[8,2,512]{2,1,0:T(2,128)S(1)}, u32[]{:S(2)}, u32[]{:S(2)}) %all-to-all-start) | async-done | bytes 32800 | tf_op jit(solution)/shard_map/all_to_all | solution.py:256
  17.3 0.0 collective-permute-done.refs_0_
  17.3 0.0 collective-permute-done.1.refs_1_
  17.3 4.9 %shard_map.119 = (bf16[128,4096]{1,0:T(8,128)(2,1)}, bf16[128,4096]{1,0:T(8,128)(2,1)}, f32[128,512]{1,0:T(8,128)S(1)}, f32[128,512]{1,0:T(8,128)S(1)}, bf16[1,2...) custom-call(bf16[128,4096]{1,0:T(8,128)(2,1)S(1)} %get-tuple-element.16.q_ref, ...), custom_call_target="tpu_custom_call" | custom-call | tf_op jit(solution)/shard_map/pallas_call | solution.py:183
  22.3 3.3 %all-to-all-start.1 = ((f32[8,2,512]{2,1,0:T(2,128)}), f32[8,2,512]{2,1,0:T(2,128)S(1)}, u32[]{:S(2)}, u32[]{:S(2)}) async-start(f32[8,2,512]{2,1,0:T(2,128)} %get-tuple-element.25), calls=%async_computation.1 | async-start | bytes 65536 | tf_op jit(solution)/shard_map/all_to_all | solution.py:269
  25.6 1.9 %collective-permute-start.2 = (bf16[2,128,512]{2,1,0:T(8,128)(2,1)S(1)}, bf16[2,128,512]{2,1,0:T(8,128)(2,1)S(1)}, u32[]{:S(2)}, u32[]{:S(2)}) collective-permute-start(bf16[2,128,512]{2,1,0:T(8,128)(2,1)S(1)} %bitcast.26), channel_id=1, source_target_pairs={{0,2},{2,0},{1,3},{3,1},{4,6},{6,4},{5,7},{7,5},{8,10},{10,8},{9,1... | collective-permute-start | bytes 786440 | tf_op jit(solution)/shard_map/ppermute | solution.py:268
  27.5 4.7 %all-to-all-done.1 = f32[8,2,512]{2,1,0:T(2,128)S(1)} async-done(((f32[8,2,512]{2,1,0:T(2,128)}), f32[8,2,512]{2,1,0:T(2,128)S(1)}, u32[]{:S(2)}, u32[]{:S(2)}) %all-to-all-start.1) | async-done | bytes 32800 | tf_op jit(solution)/shard_map/all_to_all | solution.py:269
  32.3 0.6 %fusion.4 = (f32[1,1,512]{2,1,0:T(1,128)}, f32[1,1,512]{2,1,0:T(1,128)}) fusion(f32[1,2,512]{2,1,0:T(2,128)S(1)} %bitcast.33), kind=kLoop, calls=%fused_computation.7 | loop fusion | bytes 8192 | tf_op jit(solution)/shard_map/slice | solution.py:280
  32.9 0.0 collective-permute-done.2
  32.9 0.1 convert_element_type.13
  32.9 0.9 %fusion.1 = (f32[1,1,128,512]{3,2,1,0:T(8,128)}, f32[1,1,128,512]{3,2,1,0:T(8,128)}) fusion(f32[128,512]{1,0:T(8,128)S(1)} %get-tuple-element.24, f32[2,128,512]{2,1,0:T(8,128)S(1)} %convert_element_type.13, f32[128,512]{1,0:T(8,128)S(1)} %get-tuple-element.22), kind=kLoop, calls=%fused_computation.2 | loop fusion | flops 131072 | bytes 1572864 | tf_op jit(solution)/shard_map/broadcast_in_dim | solution.py:278
  (2 shorter events, 0.0 us)
Async XLA Ops:
  0.6 16.7 %collective-permute-start = (bf16[128,512]{1,0:T(8,128)(2,1)}, bf16[128,512]{1,0:T(8,128)(2,1)S(1)}, u32[]{:S(2)}, u32[]{:S(2)}) collective-permute-start(bf16[128,512]{1,0:T(8,128)(2,1)} %bitcast.29), channel_id=1, source_target_pairs={{0,2},{2,0},{1,3},{3,1},{4,6},{6,4},{5,7},{7,5},{8,10},{10,8},{9,1... | collective-permute-start | bytes 393224 | tf_op jit(solution)/shard_map/ppermute | solution.py:254
  3.7 0.7 %copy-start.1 = (bf16[1,1,512]{2,1,0:T(2,128)(2,1)S(1)}, bf16[1,1,512]{2,1,0:T(2,128)(2,1)}, u32[]{:S(2)}) copy-start(bf16[1,1,512]{2,1,0:T(2,128)(2,1)} %param.10) | copy-start | bytes 3076
  3.7 0.7 %copy-start = (bf16[1,1,512]{2,1,0:T(2,128)(2,1)S(1)}, bf16[1,1,512]{2,1,0:T(2,128)(2,1)}, u32[]{:S(2)}) copy-start(bf16[1,1,512]{2,1,0:T(2,128)(2,1)} %param.11) | copy-start | bytes 3076
  3.7 13.7 %collective-permute-start.1 = (bf16[128,512]{1,0:T(8,128)(2,1)}, bf16[128,512]{1,0:T(8,128)(2,1)S(1)}, u32[]{:S(2)}, u32[]{:S(2)}) collective-permute-start(bf16[128,512]{1,0:T(8,128)(2,1)} %bitcast.31), channel_id=1, source_target_pairs={{0,2},{2,0},{1,3},{3,1},{4,6},{6,4},{5,7},{7,5},{8,10},{10,8},{9,1... | collective-permute-start | bytes 393224 | tf_op jit(solution)/shard_map/ppermute | solution.py:254
  5.0 12.3 %all-to-all-start = ((f32[8,2,512]{2,1,0:T(2,128)}), f32[8,2,512]{2,1,0:T(2,128)S(1)}, u32[]{:S(2)}, u32[]{:S(2)}) async-start(f32[8,2,512]{2,1,0:T(2,128)} %tile.2), calls=%async_computation | async-start | bytes 65536 | tf_op jit(solution)/shard_map/all_to_all | solution.py:256
  22.3 10.0 %all-to-all-start.1 = ((f32[8,2,512]{2,1,0:T(2,128)}), f32[8,2,512]{2,1,0:T(2,128)S(1)}, u32[]{:S(2)}, u32[]{:S(2)}) async-start(f32[8,2,512]{2,1,0:T(2,128)} %get-tuple-element.25), calls=%async_computation.1 | async-start | bytes 65536 | tf_op jit(solution)/shard_map/all_to_all | solution.py:269
  25.6 7.3 %collective-permute-start.2 = (bf16[2,128,512]{2,1,0:T(8,128)(2,1)S(1)}, bf16[2,128,512]{2,1,0:T(8,128)(2,1)S(1)}, u32[]{:S(2)}, u32[]{:S(2)}) collective-permute-start(bf16[2,128,512]{2,1,0:T(8,128)(2,1)S(1)} %bitcast.26), channel_id=1, source_target_pairs={{0,2},{2,0},{1,3},{3,1},{4,6},{6,4},{5,7},{7,5},{8,10},{10,8},{9,1... | collective-permute-start | bytes 786440 | tf_op jit(solution)/shard_map/ppermute | solution.py:268
where the time goes:
time: 34.2 us; the launch traced here: 33.8 us
  starting transfers between devices  14 us (41%)
  waiting for transfers between devices  8.11 us (24%)
  Pallas kernels  7.58 us (22%)
  local copies, waits for them, and re-layouts  1.81 us (5%)
  between operations  1.32 us (4%)
  other arithmetic  0.96 us (3%)
    all_to_all x1, starting transfers between devices, shards(): lax.all_to_all(jnp.tile(line, (everyone, 1, 1)), ('sample', 'fsdp'), spli...  5.65 us
    pallas_call x1, Pallas kernels, attend(): pl.pallas_call(functools.partial(attend_kernel, shifts, share), out_shape...  4.93 us
    all_to_all x1, waiting for transfers between devices, shards(): lax.all_to_all(dprefix, ('sample', 'fsdp'), split_axis=0, concat_axis=0,...  4.73 us
    all_to_all x1, waiting for transfers between devices, shards(): lax.all_to_all(jnp.tile(line, (everyone, 1, 1)), ('sample', 'fsdp'), spli...  3.37 us
    all_to_all x1, starting transfers between devices, shards(): lax.all_to_all(dprefix, ('sample', 'fsdp'), split_axis=0, concat_axis=0,...  3.34 us
    ppermute x1, starting transfers between devices, shards(): lax.ppermute(keys, 'fsdp', ring)  3.03 us
    pallas_call x1, Pallas kernels, prepare(): pl.pallas_call(functools.partial(prepare_kernel, comp_span), out_shape=[j...  2.65 us
    ppermute x1, starting transfers between devices, shards(): landed.append(lax.ppermute(dback[s - 1], 'fsdp', ring))  1.92 us
  transfers between devices with their start and end apart: 5, of which 2 were waited for; matrix products, arithmetic and copies ran while one was open for 4% of the time, Pallas kernels for 8%

commit v1 on v0

v1 whole, which is shorter than its diff:
```python
import functools

import jax
import jax.numpy as jnp
from jax import lax
from jax.experimental import pallas as pl
from jax.experimental.pallas import tpu as pltpu
from jax.sharding import PartitionSpec as P

HEAD_DIM = 128
LOG2E = 1.4426950408889634
UNITS = 2
PARTS = 4
VMEM_LIMIT = 24 << 20

NT = (((1,), (1,)), ((), ()))
NN = (((1,), (0,)), ((), ()))


def mm(a, b, dims=NN):
    return lax.dot_general(a, b, dims, preferred_element_type=jnp.float32)


def pad_rows(x, rows):
    if x.shape[0] == rows:
        return x
    return jnp.concatenate([x, jnp.zeros((rows - x.shape[0], x.shape[1]), x.dtype)], 0)


def geometry(q_ref, prefix, k_ref, shifts, share):
    rows = q_ref.shape[0]
    prompt = prefix.shape[0]
    padded = -(-prompt // 16) * 16
    chunk = min(rows, 256 // share)
    return rows, prompt, padded, padded + shifts * rows, chunk, k_ref.shape[1] // HEAD_DIM


def sides_of(units, padded, prefix, earlier, k_ref, v_ref):
    sides = []
    for u in range(units):
        col = slice(u * HEAD_DIM, (u + 1) * HEAD_DIM)
        pair = []
        for which, own in enumerate((k_ref, v_ref)):
            lead = pad_rows(prefix[:, which, col], padded).astype(jnp.bfloat16)
            past = [block[:, col] for block in earlier[which::2]]
            pair.append(jnp.concatenate([lead] + past + [own[:, col]], 0))
        sides.append(pair)
    return sides


def stacked(ref, u, share, part):
    return jnp.concatenate(
        [
            ref[part, (u * share + h) * HEAD_DIM : (u * share + h + 1) * HEAD_DIM]
            for h in range(share)
        ],
        0,
    )


def pieces(scores, seen, chunk, rows, prompt, padded, before, shifts):
    lead = scores[:prompt]
    back = [scores[padded + s * rows : padded + (s + 1) * rows] for s in range(shifts)]
    full = scores[before : seen - chunk]
    key = lax.broadcasted_iota(jnp.int32, (chunk, scores.shape[1]), 0)
    token = lax.rem(lax.broadcasted_iota(jnp.int32, (chunk, scores.shape[1]), 1), chunk)
    last = jnp.where(key <= token, scores[seen - chunk :], jnp.float32(-jnp.inf))
    return lead, back, full, last


def exponents(parts, top, bias, factor, padded):
    lead, back, full, last = parts
    out = [jnp.exp2(lead * factor - top)]
    if padded != lead.shape[0]:
        out.append(jnp.zeros((padded - lead.shape[0], lead.shape[1]), jnp.float32))
    out += [jnp.exp2(b * factor - (top - o)) for b, o in zip(back, bias)]
    if full.shape[0]:
        out.append(jnp.exp2(full * factor - top))
    out.append(jnp.exp2(last * factor - top))
    return jnp.concatenate(out, 0)


def biases(shifts):
    place = lax.axis_index("fsdp")
    return [
        jnp.where(place >= s + 1, jnp.float32(0.0), jnp.float32(-jnp.inf)) for s in range(shifts)
    ]


def grown(acc, new):
    if acc is None:
        return new
    old = acc[0].shape[0]
    return tuple(
        jnp.concatenate([a + n[:old], n[old:]], 0) if n.shape[0] > old else a + n
        for a, n in zip(acc, new)
    )


def pipeline(order, first, second, third):
    ahead, behind = first(*order[0]), None
    for n, (u, i) in enumerate(order):
        now = ahead
        if n + 1 < len(order):
            ahead = first(*order[n + 1])
        if behind is not None:
            third(*behind)
        behind = (u, i) + second(u, i, *now)
    third(*behind)


def travel_kernel(shifts, share, q_ref, g_ref, k_ref, v_ref, *refs):
    earlier, prefix = refs[: 2 * shifts], refs[2 * shifts]
    rest = refs[2 * shifts + 1 :]
    dback = rest[0] if shifts else None
    dprefix, stats = rest[-2:]
    rows, prompt, padded, before, chunk, units = geometry(q_ref, prefix, k_ref, shifts, share)
    steps = rows // chunk
    scale = HEAD_DIM ** -0.5
    factor = scale * LOG2E
    bias = biases(shifts)
    sides = sides_of(units, padded, prefix, earlier, k_ref, v_ref)
    acc = [None] * units

    def first(u, i):
        keys, values = sides[u]
        part = slice(i * chunk, (i + 1) * chunk)
        q, g = stacked(q_ref, u, share, part), stacked(g_ref, u, share, part)
        seen = before + (i + 1) * chunk
        return q, g, mm(keys[:seen], q, NT), mm(values[:seen], g, NT)

    def second(u, i, q, g, scores, dprob):
        seen = before + (i + 1) * chunk
        parts = pieces(scores, seen, chunk, rows, prompt, padded, before, shifts)
        lead, back, full, last = parts
        top = jnp.maximum(jnp.max(last, 0, keepdims=True), jnp.max(lead, 0, keepdims=True))
        if i:
            top = jnp.maximum(top, jnp.max(full, 0, keepdims=True))
        for s in range(shifts):
            top = jnp.maximum(top, jnp.max(back[s], 0, keepdims=True) + bias[s])
        top = top * factor
        expo = exponents(parts, top, bias, factor, padded)
        inverse = 1.0 / jnp.sum(expo, 0, keepdims=True)
        dot = jnp.sum(expo * dprob, 0, keepdims=True) * inverse
        n = u * steps + i
        stats[n, 0:1] = top
        stats[n, 1:2] = inverse
        stats[n, 2:3] = dot
        probs = expo[:before] * inverse
        sgrad = (probs * (dprob[:before] - dot)).astype(jnp.bfloat16)
        return q, g, probs.astype(jnp.bfloat16), sgrad

    def third(u, i, q, g, probs, sgrad):
        acc[u] = grown(acc[u], (mm(sgrad, q), mm(probs, g)))
        if i < steps - 1:
            return
        col = slice(u * HEAD_DIM, (u + 1) * HEAD_DIM)
        key_term, value_term = acc[u][0] * scale, acc[u][1]
        for s in range(shifts):
            at = slice(padded + s * rows, padded + (s + 1) * rows)
            dback[s, 0, :, col] = key_term[at].astype(jnp.bfloat16)
            dback[s, 1, :, col] = value_term[at].astype(jnp.bfloat16)
        dprefix[:, 0, col] = key_term[:prompt]
        dprefix[:, 1, col] = value_term[:prompt]

    pipeline([(u, i) for u in range(units) for i in range(steps)], first, second, third)


def stay_kernel(shifts, share, q_ref, g_ref, k_ref, v_ref, *refs):
    earlier, prefix, stats = refs[: 2 * shifts], refs[2 * shifts], refs[2 * shifts + 1]
    out, dq, dk, dv = refs[2 * shifts + 2 :]
    rows, prompt, padded, before, chunk, units = geometry(q_ref, prefix, k_ref, shifts, share)
    steps = rows // chunk
    scale = HEAD_DIM ** -0.5
    factor = scale * LOG2E
    bias = biases(shifts)
    sides = [
        (keys, values, keys.T, values.T)
        for keys, values in sides_of(units, padded, prefix, earlier, k_ref, v_ref)
    ]
    acc = [None] * units

    def first(u, i):
        keys, values = sides[u][:2]
        part = slice(i * chunk, (i + 1) * chunk)
        q, g = stacked(q_ref, u, share, part), stacked(g_ref, u, share, part)
        seen = before + (i + 1) * chunk
        return q, g, mm(keys[:seen], q, NT), mm(values[:seen], g, NT)

    def second(u, i, q, g, scores, dprob):
        seen = before + (i + 1) * chunk
        n = u * steps + i
        top, inverse, dot = stats[n, 0:1], stats[n, 1:2], stats[n, 2:3]
        parts = pieces(scores, seen, chunk, rows, prompt, padded, before, shifts)
        probs = exponents(parts, top, bias, factor, padded) * inverse
        sgrad = (probs * (dprob - dot)).astype(jnp.bfloat16)
        return q, g, probs.astype(jnp.bfloat16), sgrad

    def deep(left, right):
        total = None
        for at in range(0, right.shape[0], 256):
            end = min(at + 256, right.shape[0])
            term = mm(left[:, at:end], right[at:end])
            total = term if total is None else total + term
        return total

    def third(u, i, q, g, probs, sgrad):
        keys_t, values_t = sides[u][2:]
        seen = before + (i + 1) * chunk
        part = slice(i * chunk, (i + 1) * chunk)
        mixed = deep(values_t[:, :seen], probs).astype(jnp.bfloat16).T
        dquery = (deep(keys_t[:, :seen], sgrad) * scale).astype(jnp.bfloat16).T
        for h in range(share):
            c = slice((u * share + h) * HEAD_DIM, (u * share + h + 1) * HEAD_DIM)
            out[part, c] = mixed[h * chunk : (h + 1) * chunk]
            dq[part, c] = dquery[h * chunk : (h + 1) * chunk]
        acc[u] = grown(acc[u], (mm(sgrad[before:], q), mm(probs[before:], g)))
        if i == steps - 1:
            col = slice(u * HEAD_DIM, (u + 1) * HEAD_DIM)
            dk[:, col] = acc[u][0] * scale
            dv[:, col] = acc[u][1]

    pipeline([(u, i) for u in range(units) for i in range(steps)], first, second, third)


def specs_of(queries, keys, prefix):
    rows, width = queries.shape
    groups = keys.shape[1] // HEAD_DIM
    share = width // HEAD_DIM // groups
    units = UNITS if groups % UNITS == 0 else 1
    chunks = rows // min(rows, 256 // share)
    columns = share * rows // chunks
    wide = pl.BlockSpec((rows, units * share * HEAD_DIM), lambda i: (0, i))
    narrow = pl.BlockSpec((rows, units * HEAD_DIM), lambda i: (0, i))
    lead = pl.BlockSpec((prefix.shape[0], 2, units * HEAD_DIM), lambda i: (0, 0, i))
    stats = pl.BlockSpec((units * chunks, 8, columns), lambda i: (i, 0, 0))
    stats_shape = jax.ShapeDtypeStruct((groups * chunks, 8, columns), jnp.float32)
    return groups // units, units, share, wide, narrow, lead, stats, stats_shape


def travel(queries, grads, keys, values, earlier, prefix):
    steps, units, share, wide, narrow, lead, stats, stats_shape = specs_of(queries, keys, prefix)
    rows = queries.shape[0]
    shifts = len(earlier) // 2
    outs, out_specs = [], []
    if shifts:
        outs.append(jax.ShapeDtypeStruct((shifts, 2) + keys.shape, jnp.bfloat16))
        out_specs.append(pl.BlockSpec((shifts, 2, rows, units * HEAD_DIM), lambda i: (0, 0, 0, i)))
    outs += [jax.ShapeDtypeStruct(prefix.shape, jnp.float32), stats_shape]
    out_specs += [lead, stats]
    result = pl.pallas_call(
        functools.partial(travel_kernel, shifts, share),
        out_shape=outs,
        grid=(steps,),
        in_specs=[wide, wide, narrow, narrow] + [narrow] * (2 * shifts) + [lead],
        out_specs=out_specs,
        compiler_params=pltpu.CompilerParams(
            dimension_semantics=("arbitrary",), vmem_limit_bytes=VMEM_LIMIT
        ),
    )(queries, grads, keys, values, *earlier, prefix)
    return result if shifts else [None] + list(result)


def stay(queries, grads, keys, values, earlier, prefix, marks):
    steps, _, share, wide, narrow, lead, stats, _ = specs_of(queries, keys, prefix)
    shifts = len(earlier) // 2
    total = keys.shape[0] * (1 + shifts) + prefix.shape[0]
    return pl.pallas_call(
        functools.partial(stay_kernel, shifts, share),
        out_shape=[
            jax.ShapeDtypeStruct(queries.shape, jnp.bfloat16),
            jax.ShapeDtypeStruct(queries.shape, jnp.bfloat16),
            jax.ShapeDtypeStruct(keys.shape, jnp.float32),
            jax.ShapeDtypeStruct(keys.shape, jnp.float32),
        ],
        grid=(steps,),
        in_specs=[wide, wide, narrow, narrow] + [narrow] * (2 * shifts) + [lead, stats],
        out_specs=[wide, wide, narrow, narrow],
        cost_estimate=pl.CostEstimate(
            flops=10 * queries.size * total,
            bytes_accessed=8 * queries.size,
            transcendentals=queries.size // HEAD_DIM * total,
        ),
        compiler_params=pltpu.CompilerParams(
            dimension_semantics=("arbitrary",), vmem_limit_bytes=VMEM_LIMIT
        ),
    )(
        queries, grads, keys, values, *earlier, prefix,
        pltpu.with_memory_space_constraint(marks, pltpu.HBM),
    )


def prepare_kernel(comp_span, length_ref, g_ref, *refs):
    sources, g_out, targets, sems = refs[:3], refs[3], refs[4:7], refs[7]
    copies = [pltpu.make_async_copy(a, b, sems.at[n]) for n, (a, b) in enumerate(zip(sources, targets))]

    @pl.when(pl.program_id(0) == 0)
    def _():
        for copy in copies:
            copy.start()

    rows, width = g_ref.shape
    length = length_ref[0, 0]
    ratio = jnp.float32(comp_span) / length.astype(jnp.float32)
    token = lax.axis_index("fsdp") * rows + lax.broadcasted_iota(jnp.int32, (rows, HEAD_DIM), 0)
    weight = jnp.where(token < length, ratio, jnp.float32(0.0))
    for at in range(0, width, HEAD_DIM):
        c = slice(at, at + HEAD_DIM)
        g_out[:, c] = (g_ref[:, c].astype(jnp.float32) * weight).astype(jnp.bfloat16)

    @pl.when(pl.program_id(0) == pl.num_programs(0) - 1)
    def _():
        for copy in copies:
            copy.wait()


def prepare(lengths, queries, grads, keys, values, comp_span):
    rows, width = grads.shape
    parts = PARTS if width % (PARTS * HEAD_DIM) == 0 else 1
    wide = pl.BlockSpec((rows, width // parts), lambda i: (0, i))
    whole = pl.BlockSpec(memory_space=pl.ANY)
    arrays = [pltpu.with_memory_space_constraint(x, pltpu.HBM) for x in (grads, queries, keys, values)]
    moved = 2 * 2 * (queries.size + grads.size + keys.size + values.size)
    g, q, k, v = pl.pallas_call(
        functools.partial(prepare_kernel, comp_span),
        out_shape=[jax.ShapeDtypeStruct(x.shape, x.dtype) for x in arrays],
        grid=(parts,),
        in_specs=[pl.BlockSpec(memory_space=pltpu.SMEM), wide, whole, whole, whole],
        out_specs=[wide, whole, whole, whole],
        scratch_shapes=[pltpu.SemaphoreType.DMA((3,))],
        cost_estimate=pl.CostEstimate(flops=grads.size, bytes_accessed=moved, transcendentals=0),
        compiler_params=pltpu.CompilerParams(
            dimension_semantics=("arbitrary",), vmem_limit_bytes=VMEM_LIMIT
        ),
    )(lengths, *arrays)
    return q, g, k, v


def shards(
    queries, completion_keys, completion_values, prompt_keys, prompt_values, output_grad, lengths
):
    fsdp = lax.axis_size("fsdp")
    everyone = fsdp * lax.axis_size("sample")
    rows = queries.shape[2]
    keys, values = completion_keys[0, 0], completion_values[0, 0]
    earlier = []
    for s in range(1, fsdp):
        ring = [(i, (i + s) % fsdp) for i in range(fsdp)]
        earlier += [lax.ppermute(keys, "fsdp", ring), lax.ppermute(values, "fsdp", ring)]
    line = jnp.stack([prompt_keys[0], prompt_values[0]], 1).astype(jnp.float32)
    prefix = lax.all_to_all(
        jnp.tile(line, (everyone, 1, 1)),
        ("sample", "fsdp"),
        split_axis=0,
        concat_axis=0,
        tiled=True,
    )
    q, g, k, v = prepare(lengths, queries[0, 0], output_grad[0, 0], keys, values, rows * fsdp)
    dback, dprefix, marks = travel(q, g, k, v, earlier, prefix)
    landed = []
    for s in range(1, fsdp):
        ring = [(i, (i - s) % fsdp) for i in range(fsdp)]
        landed.append(lax.ppermute(dback[s - 1], "fsdp", ring))
    shares = lax.all_to_all(dprefix, ("sample", "fsdp"), split_axis=0, concat_axis=0, tiled=True)
    out, dq, dk, dv = stay(q, g, k, v, earlier, prefix, marks)
    for block in landed:
        block = block.astype(jnp.float32)
        dk, dv = dk + block[0], dv + block[1]
    total = jnp.sum(shares.reshape((everyone, -1) + shares.shape[1:]), 0)
    return (
        out[None, None],
        dq[None, None],
        dk[None, None],
        dv[None, None],
        total[None, :, 0],
        total[None, :, 1],
    )


def solution(mesh):
    wide = P(("groups", "prompt"), "sample", "fsdp", None)
    lead = P(("groups", "prompt"), ("sample", "fsdp"), None)
    in_specs = (wide, wide, wide, lead, lead, wide, P(("groups", "prompt"), "sample"))
    out_specs = (wide, wide, wide, wide, lead, lead)
    return jax.shard_map(shards, mesh=mesh, in_specs=in_specs, out_specs=out_specs, check_vma=False)
```

time: 34.2 us -> 34.4 us (level)
  waiting for transfers between devices: 8.11 us -> 3.48 us
  Pallas kernels: 7.58 us -> 10.8 us
  other arithmetic: 0.96 us -> 1.91 us
  local copies, waits for them, and re-layouts: 1.81 us -> 2.47 us
    all_to_all x1, waiting for transfers between devices: 4.73 us -> 0.09 us  [shards(): lax.all_to_all(dprefix, ('sample', 'fsdp'), split_axis=0, concat_axis=0,...]
    pallas_call x1 -> x2, Pallas kernels: 4.93 us -> 8.13 us  [the longest x1 4.63 us: stay(): pl.pallas_call(functools.partial(stay_kernel, shifts, share), out_shape=[...]
    convert_element_type x1, other arithmetic: 0.05 us -> 1 us  [shards(): block = block.astype(jnp.float32)]
    unnamed x4 -> x6, local copies, waits for them, and re-layouts: 0.6 us -> 1.25 us
  transfers between devices with their start and end apart: 5 -> 5, of which waited for: 2 -> 2; matrix products, arithmetic and copies ran while one was open for 4% -> 4% of each run, Pallas kernels for 8% -> 21%
where the time goes in v1:
time: 34.4 us; the launch traced here: 34 us
  starting transfers between devices  14 us (41%)
  Pallas kernels  10.8 us (31%)
  waiting for transfers between devices  3.48 us (10%)
  local copies, waits for them, and re-layouts  2.47 us (7%)
  other arithmetic  1.91 us (6%)
  between operations  1.32 us (4%)
    all_to_all x1, starting transfers between devices, shards(): lax.all_to_all(jnp.tile(line, (everyone, 1, 1)), ('sample', 'fsdp'), spli...  5.65 us
    pallas_call x1, Pallas kernels, stay(): pl.pallas_call(functools.partial(stay_kernel, shifts, share), out_shape=[...  4.63 us
    pallas_call x1, Pallas kernels, travel(): pl.pallas_call(functools.partial(travel_kernel, shifts, share), out_shape...  3.5 us
    all_to_all x1, waiting for transfers between devices, shards(): lax.all_to_all(jnp.tile(line, (everyone, 1, 1)), ('sample', 'fsdp'), spli...  3.37 us
    all_to_all x1, starting transfers between devices, shards(): lax.all_to_all(dprefix, ('sample', 'fsdp'), split_axis=0, concat_axis=0,...  3.34 us
    ppermute x1, starting transfers between devices, shards(): lax.ppermute(keys, 'fsdp', ring)  3.03 us
    pallas_call x1, Pallas kernels, prepare(): pl.pallas_call(functools.partial(prepare_kernel, comp_span), out_shape=[j...  2.65 us
    ppermute x1, starting transfers between devices, shards(): landed.append(lax.ppermute(dback[s - 1], 'fsdp', ring))  1.92 us
  transfers between devices with their start and end apart: 5, of which 2 were waited for; matrix products, arithmetic and copies ran while one was open for 4% of the time, Pallas kernels for 21%

profile of v1, /device:TPU:0, one launch (start us, length us, event | category | flops | bytes accessed | tf_op | source)
XLA Modules:
  0.0 34.0 jit_solution(15046697043448459001)
XLA Ops:
  0.6 3.0 %collective-permute-start = (bf16[128,512]{1,0:T(8,128)(2,1)}, bf16[128,512]{1,0:T(8,128)(2,1)S(1)}, u32[]{:S(2)}, u32[]{:S(2)}) collective-permute-start(bf16[128,512]{1,0:T(8,128)(2,1)} %bitcast.29), channel_id=1, source_target_pairs={{0,2},{2,0},{1,3},{3,1},{4,6},{6,4},{5,7},{7,5},{8,10},{10,8},{9,1... | collective-permute-start | bytes 393224 | tf_op jit(solution)/shard_map/ppermute | solution.py:349
  3.7 0.0 copy-start.2
  3.7 0.0 copy-start.1
  3.7 0.1 collective-permute-start.1
  3.8 0.6 %copy-done.2 = bf16[1,1,512]{2,1,0:T(2,128)(2,1)S(1)} copy-done((bf16[1,1,512]{2,1,0:T(2,128)(2,1)S(1)}, bf16[1,1,512]{2,1,0:T(2,128)(2,1)}, u32[]{:S(2)}) %copy-start.2) | copy-done | bytes 1048
  4.3 0.0 copy-done.1
  4.4 0.6 %tile.2 = f32[8,2,512]{2,1,0:T(2,128)} broadcast(f32[2,512]{1,0:T(2,128)S(1)} %maximum_convert_fusion), dimensions={1,2} | broadcast | bytes 36864 | tf_op jit(solution)/shard_map/tile | solution.py:352
  5.0 5.7 %all-to-all-start = ((f32[8,2,512]{2,1,0:T(2,128)}), f32[8,2,512]{2,1,0:T(2,128)S(1)}, u32[]{:S(2)}, u32[]{:S(2)}) async-start(f32[8,2,512]{2,1,0:T(2,128)} %tile.2), calls=%async_computation | async-start | bytes 65536 | tf_op jit(solution)/shard_map/all_to_all | solution.py:351
  11.3 2.7 %shard_map.118 = (bf16[128,4096]{1,0:T(8,128)(2,1)S(1)}, bf16[128,4096]{1,0:T(8,128)(2,1)S(1)}, bf16[128,512]{1,0:T(8,128)(2,1)S(1)}, bf16[128,512]{1,0:T(8,128)(2,1)S(1)}) custom-call(s32[1,1]{1,0:T(1,128)S(6)} %copy.13.length_ref, bf16[128,4096]{1,0:T(8,128)(2,1)} %bitcast.27, bf16[128,4096]{1,0:T(8,128)(2,1)} %bitcast.28, bf16[128,512]{1,0:T(8,128)(2,1)} %bitcast.30, ...), custom_call_target="tpu_custom_call" | custom-call | flops 524288 | bytes 4718592 | tf_op jit(solution)/shard_map/pallas_call | solution.py:324
  14.0 3.4 %all-to-all-done.refs_2_ = f32[8,2,512]{2,1,0:T(2,128)S(1)} async-done(((f32[8,2,512]{2,1,0:T(2,128)}), f32[8,2,512]{2,1,0:T(2,128)S(1)}, u32[]{:S(2)}, u32[]{:S(2)}) %all-to-all-start) | async-done | bytes 32800 | tf_op jit(solution)/shard_map/all_to_all | solution.py:351
  17.3 0.0 collective-permute-done.refs_0_
  17.3 0.0 collective-permute-done.1.refs_1_
  17.3 3.5 %shard_map.119 = (bf16[1,2,128,512]{3,2,1,0:T(8,128)(2,1)S(1)}, f32[8,2,512]{2,1,0:T(2,128)}, f32[16,8,256]{2,1,0:T(8,128)S(1)}) custom-call(bf16[128,4096]{1,0:T(8,128)(2,1)S(1)} %get-tuple-element.17.q_ref, bf16[128,4096]{1,0:T(8,128)(2,1)S(1)} %get-tuple-element.18.g_ref, bf16[128,512]{1,0:T(8,128)(2,1)S(1)} %get-tuple-element.19.k_ref, ...), custom_call_target="tpu_custom_call" | custom-call | tf_op jit(solution)/shard_map/pallas_call | solution.py:251
  20.8 0.0 copy-start
  20.8 0.7 %copy-done = f32[16,8,256]{2,1,0:T(8,128)} copy-done((f32[16,8,256]{2,1,0:T(8,128)}, f32[16,8,256]{2,1,0:T(8,128)S(1)}, u32[]{:S(2)}) %copy-start) | copy-done | bytes 131096
  21.5 3.3 %all-to-all-start.1 = ((f32[8,2,512]{2,1,0:T(2,128)}), f32[8,2,512]{2,1,0:T(2,128)S(1)}, u32[]{:S(2)}, u32[]{:S(2)}) async-start(f32[8,2,512]{2,1,0:T(2,128)} %get-tuple-element.27), calls=%async_computation.1 | async-start | bytes 65536 | tf_op jit(solution)/shard_map/all_to_all | solution.py:364
  24.8 1.9 %collective-permute-start.2 = (bf16[2,128,512]{2,1,0:T(8,128)(2,1)S(1)}, bf16[2,128,512]{2,1,0:T(8,128)(2,1)}, u32[]{:S(2)}, u32[]{:S(2)}) collective-permute-start(bf16[2,128,512]{2,1,0:T(8,128)(2,1)S(1)} %bitcast.26), channel_id=1, source_target_pairs={{0,2},{2,0},{1,3},{3,1},{4,6},{6,4},{5,7},{7,5},{8,10},{10,8},{9,1... | collective-permute-start | bytes 786440 | tf_op jit(solution)/shard_map/ppermute | solution.py:363
  26.8 4.6 %shard_map.120 = (bf16[128,4096]{1,0:T(8,128)(2,1)}, bf16[128,4096]{1,0:T(8,128)(2,1)}, f32[128,512]{1,0:T(8,128)S(1)}, f32[128,512]{1,0:T(8,128)S(1)}) custom-call(bf16[128,4096]{1,0:T(8,128)(2,1)S(1)} %get-tuple-element.17.q_ref, bf16[128,4096]{1,0:T(8,128)(2,1)S(1)} %get-tuple-element.18.g_ref, bf16[128,512]{1,0:T(8,128)(2,1)S(1)} %get-tuple-element.19.k_ref, ...), custom_call_target="tpu_custom_call" | custom-call | flops 1384120320 | bytes 4194304 | tf_op jit(solution)/shard_map/pallas_call | solution.py:268
  31.4 0.1 all-to-all-done.1
  31.5 0.6 %fusion.4 = (f32[1,1,512]{2,1,0:T(1,128)}, f32[1,1,512]{2,1,0:T(1,128)}) fusion(f32[1,2,512]{2,1,0:T(2,128)S(1)} %bitcast.33), kind=kLoop, calls=%fused_computation.7 | loop fusion | bytes 8192 | tf_op jit(solution)/shard_map/slice | solution.py:376
  32.1 0.0 collective-permute-done.2
  32.1 1.0 %convert_element_type.13 = f32[2,128,512]{2,1,0:T(8,128)S(1)} convert(bf16[2,128,512]{2,1,0:T(8,128)(2,1)} %collective-permute-done.2) | non-fusion elementwise | flops 131072 | bytes 786432 | tf_op jit(solution)/shard_map/convert_element_type | solution.py:367
  33.1 0.9 %fusion.1 = (f32[1,1,128,512]{3,2,1,0:T(8,128)}, f32[1,1,128,512]{3,2,1,0:T(8,128)}) fusion(f32[128,512]{1,0:T(8,128)S(1)} %get-tuple-element.26, f32[2,128,512]{2,1,0:T(8,128)S(1)} %convert_element_type.13, f32[128,512]{1,0:T(8,128)S(1)} %get-tuple-element.24), kind=kLoop, calls=%fused_computation.2 | loop fusion | flops 131072 | bytes 1572864 | tf_op jit(solution)/shard_map/broadcast_in_dim | solution.py:374
  (2 shorter events, 0.0 us)
Async XLA Ops:
  0.6 16.7 %collective-permute-start = (bf16[128,512]{1,0:T(8,128)(2,1)}, bf16[128,512]{1,0:T(8,128)(2,1)S(1)}, u32[]{:S(2)}, u32[]{:S(2)}) collective-permute-start(bf16[128,512]{1,0:T(8,128)(2,1)} %bitcast.29), channel_id=1, source_target_pairs={{0,2},{2,0},{1,3},{3,1},{4,6},{6,4},{5,7},{7,5},{8,10},{10,8},{9,1... | collective-permute-start | bytes 393224 | tf_op jit(solution)/shard_map/ppermute | solution.py:349
  3.7 0.7 %copy-start.2 = (bf16[1,1,512]{2,1,0:T(2,128)(2,1)S(1)}, bf16[1,1,512]{2,1,0:T(2,128)(2,1)}, u32[]{:S(2)}) copy-start(bf16[1,1,512]{2,1,0:T(2,128)(2,1)} %param.10) | copy-start | bytes 3076
  3.7 0.7 %copy-start.1 = (bf16[1,1,512]{2,1,0:T(2,128)(2,1)S(1)}, bf16[1,1,512]{2,1,0:T(2,128)(2,1)}, u32[]{:S(2)}) copy-start(bf16[1,1,512]{2,1,0:T(2,128)(2,1)} %param.11) | copy-start | bytes 3076
  3.7 13.7 %collective-permute-start.1 = (bf16[128,512]{1,0:T(8,128)(2,1)}, bf16[128,512]{1,0:T(8,128)(2,1)S(1)}, u32[]{:S(2)}, u32[]{:S(2)}) collective-permute-start(bf16[128,512]{1,0:T(8,128)(2,1)} %bitcast.31), channel_id=1, source_target_pairs={{0,2},{2,0},{1,3},{3,1},{4,6},{6,4},{5,7},{7,5},{8,10},{10,8},{9,1... | collective-permute-start | bytes 393224 | tf_op jit(solution)/shard_map/ppermute | solution.py:349
  5.0 12.3 %all-to-all-start = ((f32[8,2,512]{2,1,0:T(2,128)}), f32[8,2,512]{2,1,0:T(2,128)S(1)}, u32[]{:S(2)}, u32[]{:S(2)}) async-start(f32[8,2,512]{2,1,0:T(2,128)} %tile.2), calls=%async_computation | async-start | bytes 65536 | tf_op jit(solution)/shard_map/all_to_all | solution.py:351
  20.8 0.7 %copy-start = (f32[16,8,256]{2,1,0:T(8,128)}, f32[16,8,256]{2,1,0:T(8,128)S(1)}, u32[]{:S(2)}) copy-start(f32[16,8,256]{2,1,0:T(8,128)S(1)} %get-tuple-element.21.refs_3_) | copy-start | bytes 393220
  21.5 10.0 %all-to-all-start.1 = ((f32[8,2,512]{2,1,0:T(2,128)}), f32[8,2,512]{2,1,0:T(2,128)S(1)}, u32[]{:S(2)}, u32[]{:S(2)}) async-start(f32[8,2,512]{2,1,0:T(2,128)} %get-tuple-element.27), calls=%async_computation.1 | async-start | bytes 65536 | tf_op jit(solution)/shard_map/all_to_all | solution.py:364
  24.8 7.3 %collective-permute-start.2 = (bf16[2,128,512]{2,1,0:T(8,128)(2,1)S(1)}, bf16[2,128,512]{2,1,0:T(8,128)(2,1)}, u32[]{:S(2)}, u32[]{:S(2)}) collective-permute-start(bf16[2,128,512]{2,1,0:T(8,128)(2,1)S(1)} %bitcast.26), channel_id=1, source_target_pairs={{0,2},{2,0},{1,3},{3,1},{4,6},{6,4},{5,7},{7,5},{8,10},{10,8},{9,1... | collective-permute-start | bytes 786440 | tf_op jit(solution)/shard_map/ppermute | solution.py:363

commit v2 on v1

--- a/solution.py
+++ b/solution.py
@@ -234,7 +234,7 @@
     narrow = pl.BlockSpec((rows, units * HEAD_DIM), lambda i: (0, i))
     lead = pl.BlockSpec((prefix.shape[0], 2, units * HEAD_DIM), lambda i: (0, 0, i))
     stats = pl.BlockSpec((units * chunks, 8, columns), lambda i: (i, 0, 0))
-    stats_shape = jax.ShapeDtypeStruct((groups * chunks, 8, columns), jnp.float32)
+    stats_shape = pltpu.HBM((groups * chunks, 8, columns), jnp.float32)
     return groups // units, units, share, wide, narrow, lead, stats, stats_shape
 
 
@@ -336,6 +336,32 @@
     return q, g, k, v
 
 
+def finish_kernel(count, dk, dv, shares, *refs):
+    blocks, (dk_out, dv_out, lead_k, lead_v) = refs[:count], refs[count:]
+    key_term, value_term = dk[...], dv[...]
+    for block in blocks:
+        key_term += block[0].astype(jnp.float32)
+        value_term += block[1].astype(jnp.float32)
+    dk_out[...] = key_term
+    dv_out[...] = value_term
+    here = lead_k.shape[0]
+    total = shares[:here]
+    for at in range(here, shares.shape[0], here):
+        total += shares[at : at + here]
+    lead_k[...] = total[:, 0]
+    lead_v[...] = total[:, 1]
+
+
+def finish(dk, dv, shares, landed, here):
+    lead = jax.ShapeDtypeStruct((here, shares.shape[2]), jnp.float32)
+    whole = jax.ShapeDtypeStruct(dk.shape, jnp.float32)
+    return pl.pallas_call(
+        functools.partial(finish_kernel, len(landed)),
+        out_shape=[whole, whole, lead, lead],
+        compiler_params=pltpu.CompilerParams(vmem_limit_bytes=VMEM_LIMIT),
+    )(dk, dv, shares, *landed)
+
+
 def shards(
     queries, completion_keys, completion_values, prompt_keys, prompt_values, output_grad, lengths
 ):
@@ -346,15 +372,11 @@
     earlier = []
     for s in range(1, fsdp):
         ring = [(i, (i + s) % fsdp) for i in range(fsdp)]
-        earlier += [lax.ppermute(keys, "fsdp", ring), lax.ppermute(values, "fsdp", ring)]
+        earlier.append(lax.ppermute(keys, "fsdp", ring))
+        earlier.append(lax.ppermute(values, "fsdp", ring))
     line = jnp.stack([prompt_keys[0], prompt_values[0]], 1).astype(jnp.float32)
-    prefix = lax.all_to_all(
-        jnp.tile(line, (everyone, 1, 1)),
-        ("sample", "fsdp"),
-        split_axis=0,
-        concat_axis=0,
-        tiled=True,
-    )
+    line = jnp.tile(line, (everyone, 1, 1))
+    prefix = lax.all_to_all(line, ("sample", "fsdp"), split_axis=0, concat_axis=0, tiled=True)
     q, g, k, v = prepare(lengths, queries[0, 0], output_grad[0, 0], keys, values, rows * fsdp)
     dback, dprefix, marks = travel(q, g, k, v, earlier, prefix)
     landed = []
@@ -363,17 +385,14 @@
         landed.append(lax.ppermute(dback[s - 1], "fsdp", ring))
     shares = lax.all_to_all(dprefix, ("sample", "fsdp"), split_axis=0, concat_axis=0, tiled=True)
     out, dq, dk, dv = stay(q, g, k, v, earlier, prefix, marks)
-    for block in landed:
-        block = block.astype(jnp.float32)
-        dk, dv = dk + block[0], dv + block[1]
-    total = jnp.sum(shares.reshape((everyone, -1) + shares.shape[1:]), 0)
+    dk, dv, lead_k, lead_v = finish(dk, dv, shares, landed, prompt_keys.shape[1])
     return (
         out[None, None],
         dq[None, None],
         dk[None, None],
         dv[None, None],
-        total[None, :, 0],
-        total[None, :, 1],
+        lead_k[None],
+        lead_v[None],
     )
 
 

time: 34.4 us -> 32.5 us (0.945)
  other arithmetic: 1.91 us -> 0.01 us
  waiting for transfers between devices: 3.48 us -> 5.35 us
  starting transfers between devices: 14 us -> 12.6 us
  local copies, waits for them, and re-layouts: 2.47 us -> 1.22 us
  Pallas kernels: 10.8 us -> 11.7 us
    all_to_all x1, waiting for transfers between devices: 0.09 us -> 1.97 us  [shards(): lax.all_to_all(dprefix, ('sample', 'fsdp'), split_axis=0, concat_axis=0,...]
    ppermute x1, starting transfers between devices: 1.92 us -> 0.47 us  [shards(): landed.append(lax.ppermute(dback[s - 1], 'fsdp', ring))]
    convert_element_type x1 -> x0, other arithmetic: 1 us -> none  [shards(): block = block.astype(jnp.float32)]
    broadcast_in_dim x1 -> x0, other arithmetic: 0.88 us -> none  [shards(): dv[None, None]]
    pallas_call x0 -> x1, Pallas kernels: none -> 0.84 us  [finish(): pl.pallas_call(functools.partial(finish_kernel, len(landed)), out_shape=[...]
    unnamed x6 -> x4, local copies, waits for them, and re-layouts: 1.25 us -> 0.6 us
    slice x1 -> x0, local copies, waits for them, and re-layouts: 0.59 us -> none  [shards(): total[None, :, 1]]
  transfers between devices with their start and end apart: 5 -> 5, of which waited for: 2 -> 2; matrix products, arithmetic and copies ran while one was open for 4% -> 2% of each run, Pallas kernels for 21% -> 23%
where the time goes in v2:
time: 32.5 us; the launch traced here: 32.2 us
  starting transfers between devices  12.6 us (39%)
  Pallas kernels  11.7 us (36%)
  waiting for transfers between devices  5.35 us (16%)
  between operations  1.31 us (4%)
  local copies, waits for them, and re-layouts  1.22 us (4%)
    all_to_all x1, starting transfers between devices, shards(): lax.all_to_all(line, ('sample', 'fsdp'), split_axis=0, concat_axis=0, til...  5.65 us
    pallas_call x1, Pallas kernels, stay(): pl.pallas_call(functools.partial(stay_kernel, shifts, share), out_shape=[...  4.65 us
    pallas_call x1, Pallas kernels, travel(): pl.pallas_call(functools.partial(travel_kernel, shifts, share), out_shape...  3.55 us
    all_to_all x1, waiting for transfers between devices, shards(): lax.all_to_all(line, ('sample', 'fsdp'), split_axis=0, concat_axis=0, til...  3.37 us
    all_to_all x1, starting transfers between devices, shards(): lax.all_to_all(dprefix, ('sample', 'fsdp'), split_axis=0, concat_axis=0,...  3.32 us
    ppermute x1, starting transfers between devices, shards(): earlier.append(lax.ppermute(keys, 'fsdp', ring))  3.03 us
    pallas_call x1, Pallas kernels, prepare(): pl.pallas_call(functools.partial(prepare_kernel, comp_span), out_shape=[j...  2.65 us
    all_to_all x1, waiting for transfers between devices, shards(): lax.all_to_all(dprefix, ('sample', 'fsdp'), split_axis=0, concat_axis=0,...  1.97 us
  transfers between devices with their start and end apart: 5, of which 2 were waited for; matrix products, arithmetic and copies ran while one was open for 2% of the time, Pallas kernels for 23%

profile of v2, /device:TPU:0, one launch (start us, length us, event | category | flops | bytes accessed | tf_op | source)
XLA Modules:
  0.0 32.2 jit_solution(7118648350888441174)
XLA Ops:
  0.6 3.0 %collective-permute-start = (bf16[128,512]{1,0:T(8,128)(2,1)}, bf16[128,512]{1,0:T(8,128)(2,1)S(1)}, u32[]{:S(2)}, u32[]{:S(2)}) collective-permute-start(bf16[128,512]{1,0:T(8,128)(2,1)} %bitcast.15), channel_id=1, source_target_pairs={{0,2},{2,0},{1,3},{3,1},{4,6},{6,4},{5,7},{7,5},{8,10},{10,8},{9,1... | collective-permute-start | bytes 393224 | tf_op jit(solution)/shard_map/ppermute | solution.py:375
  3.7 0.0 copy-start.1
  3.7 0.0 copy-start
  3.7 0.1 collective-permute-start.1
  3.8 0.6 %copy-done.1 = bf16[1,1,512]{2,1,0:T(2,128)(2,1)S(1)} copy-done((bf16[1,1,512]{2,1,0:T(2,128)(2,1)S(1)}, bf16[1,1,512]{2,1,0:T(2,128)(2,1)}, u32[]{:S(2)}) %copy-start.1) | copy-done | bytes 1048
  4.3 0.0 copy-done
  4.4 0.6 %tile.2 = f32[8,2,512]{2,1,0:T(2,128)} broadcast(f32[2,512]{1,0:T(2,128)S(1)} %maximum_convert_fusion), dimensions={1,2} | broadcast | bytes 36864 | tf_op jit(solution)/shard_map/tile | solution.py:378
  5.0 5.7 %all-to-all-start = ((f32[8,2,512]{2,1,0:T(2,128)}), f32[8,2,512]{2,1,0:T(2,128)S(1)}, u32[]{:S(2)}, u32[]{:S(2)}) async-start(f32[8,2,512]{2,1,0:T(2,128)} %tile.2), calls=%async_computation | async-start | bytes 65536 | tf_op jit(solution)/shard_map/all_to_all | solution.py:379
  11.3 2.7 %shard_map.118 = (bf16[128,4096]{1,0:T(8,128)(2,1)S(1)}, bf16[128,4096]{1,0:T(8,128)(2,1)S(1)}, bf16[128,512]{1,0:T(8,128)(2,1)S(1)}, bf16[128,512]{1,0:T(8,128)(2,1)S(1)}) custom-call(s32[1,1]{1,0:T(1,128)S(6)} %copy.13.length_ref, bf16[128,4096]{1,0:T(8,128)(2,1)} %bitcast.13, bf16[128,4096]{1,0:T(8,128)(2,1)} %bitcast.14, bf16[128,512]{1,0:T(8,128)(2,1)} %bitcast.16, ...), custom_call_target="tpu_custom_call" | custom-call | flops 524288 | bytes 4718592 | tf_op jit(solution)/shard_map/pallas_call | solution.py:324
  14.0 3.4 %all-to-all-done.refs_2_ = f32[8,2,512]{2,1,0:T(2,128)S(1)} async-done(((f32[8,2,512]{2,1,0:T(2,128)}), f32[8,2,512]{2,1,0:T(2,128)S(1)}, u32[]{:S(2)}, u32[]{:S(2)}) %all-to-all-start) | async-done | bytes 32800 | tf_op jit(solution)/shard_map/all_to_all | solution.py:379
  17.3 0.0 collective-permute-done.refs_0_
  17.3 0.0 collective-permute-done.1.refs_1_
  17.3 3.6 %shard_map.119 = (bf16[1,2,128,512]{3,2,1,0:T(8,128)(2,1)}, f32[8,2,512]{2,1,0:T(2,128)}, f32[16,8,256]{2,1,0:T(8,128)}) custom-call(bf16[128,4096]{1,0:T(8,128)(2,1)S(1)} %get-tuple-element.21.q_ref, bf16[128,4096]{1,0:T(8,128)(2,1)S(1)} %get-tuple-element.22.g_ref, bf16[128,512]{1,0:T(8,128)(2,1)S(1)} %get-tuple-element.23.k_ref, ...), custom_call_target="tpu_custom_call" | custom-call | tf_op jit(solution)/shard_map/pallas_call | solution.py:251
  20.9 0.5 %collective-permute-start.2 = (bf16[2,128,512]{2,1,0:T(8,128)(2,1)}, bf16[2,128,512]{2,1,0:T(8,128)(2,1)S(1)}, u32[]{:S(2)}, u32[]{:S(2)}) collective-permute-start(bf16[2,128,512]{2,1,0:T(8,128)(2,1)} %bitcast.8), channel_id=1, source_target_pairs={{0,2},{2,0},{1,3},{3,1},{4,6},{6,4},{5,7},{7,5},{8,10},{10,8},{9,1... | collective-permute-start | bytes 786440 | tf_op jit(solution)/shard_map/ppermute | solution.py:385
  21.4 3.3 %all-to-all-start.1 = ((f32[8,2,512]{2,1,0:T(2,128)}), f32[8,2,512]{2,1,0:T(2,128)S(1)}, u32[]{:S(2)}, u32[]{:S(2)}) async-start(f32[8,2,512]{2,1,0:T(2,128)} %get-tuple-element.30), calls=%async_computation.1 | async-start | bytes 65536 | tf_op jit(solution)/shard_map/all_to_all | solution.py:386
  24.7 4.7 %shard_map.120 = (bf16[128,4096]{1,0:T(8,128)(2,1)}, bf16[128,4096]{1,0:T(8,128)(2,1)}, f32[128,512]{1,0:T(8,128)S(1)}, f32[128,512]{1,0:T(8,128)S(1)}) custom-call(bf16[128,4096]{1,0:T(8,128)(2,1)S(1)} %get-tuple-element.21.q_ref, bf16[128,4096]{1,0:T(8,128)(2,1)S(1)} %get-tuple-element.22.g_ref, bf16[128,512]{1,0:T(8,128)(2,1)S(1)} %get-tuple-element.23.k_ref, ...), custom_call_target="tpu_custom_call" | custom-call | flops 1384120320 | bytes 4194304 | tf_op jit(solution)/shard_map/pallas_call | solution.py:268
  29.4 2.0 %all-to-all-done.1.shares = f32[8,2,512]{2,1,0:T(2,128)S(1)} async-done(((f32[8,2,512]{2,1,0:T(2,128)}), f32[8,2,512]{2,1,0:T(2,128)S(1)}, u32[]{:S(2)}, u32[]{:S(2)}) %all-to-all-start.1) | async-done | bytes 32800 | tf_op jit(solution)/shard_map/all_to_all | solution.py:386
  31.3 0.0 collective-permute-done.2.refs_0_
  31.3 0.8 %shard_map.121 = (f32[128,512]{1,0:T(8,128)}, f32[128,512]{1,0:T(8,128)}, f32[1,512]{1,0:T(1,128)}, f32[1,512]{1,0:T(1,128)}) custom-call(f32[128,512]{1,0:T(8,128)S(1)} %get-tuple-element.28.dk, f32[128,512]{1,0:T(8,128)S(1)} %get-tuple-element.29.dv, f32[8,2,512]{2,1,0:T(2,128)S(1)} %all-to-all-done.1.shares, ...), custom_call_target="tpu_custom_call" | custom-call | tf_op jit(solution)/shard_map/pallas_call | solution.py:358
  (1 shorter events, 0.0 us)
Async XLA Ops:
  0.6 16.7 %collective-permute-start = (bf16[128,512]{1,0:T(8,128)(2,1)}, bf16[128,512]{1,0:T(8,128)(2,1)S(1)}, u32[]{:S(2)}, u32[]{:S(2)}) collective-permute-start(bf16[128,512]{1,0:T(8,128)(2,1)} %bitcast.15), channel_id=1, source_target_pairs={{0,2},{2,0},{1,3},{3,1},{4,6},{6,4},{5,7},{7,5},{8,10},{10,8},{9,1... | collective-permute-start | bytes 393224 | tf_op jit(solution)/shard_map/ppermute | solution.py:375
  3.7 0.7 %copy-start.1 = (bf16[1,1,512]{2,1,0:T(2,128)(2,1)S(1)}, bf16[1,1,512]{2,1,0:T(2,128)(2,1)}, u32[]{:S(2)}) copy-start(bf16[1,1,512]{2,1,0:T(2,128)(2,1)} %param.10) | copy-start | bytes 3076
  3.7 0.7 %copy-start = (bf16[1,1,512]{2,1,0:T(2,128)(2,1)S(1)}, bf16[1,1,512]{2,1,0:T(2,128)(2,1)}, u32[]{:S(2)}) copy-start(bf16[1,1,512]{2,1,0:T(2,128)(2,1)} %param.11) | copy-start | bytes 3076
  3.7 13.7 %collective-permute-start.1 = (bf16[128,512]{1,0:T(8,128)(2,1)}, bf16[128,512]{1,0:T(8,128)(2,1)S(1)}, u32[]{:S(2)}, u32[]{:S(2)}) collective-permute-start(bf16[128,512]{1,0:T(8,128)(2,1)} %bitcast.17), channel_id=1, source_target_pairs={{0,2},{2,0},{1,3},{3,1},{4,6},{6,4},{5,7},{7,5},{8,10},{10,8},{9,1... | collective-permute-start | bytes 393224 | tf_op jit(solution)/shard_map/ppermute | solution.py:376
  5.0 12.3 %all-to-all-start = ((f32[8,2,512]{2,1,0:T(2,128)}), f32[8,2,512]{2,1,0:T(2,128)S(1)}, u32[]{:S(2)}, u32[]{:S(2)}) async-start(f32[8,2,512]{2,1,0:T(2,128)} %tile.2), calls=%async_computation | async-start | bytes 65536 | tf_op jit(solution)/shard_map/all_to_all | solution.py:379
  20.9 10.4 %collective-permute-start.2 = (bf16[2,128,512]{2,1,0:T(8,128)(2,1)}, bf16[2,128,512]{2,1,0:T(8,128)(2,1)S(1)}, u32[]{:S(2)}, u32[]{:S(2)}) collective-permute-start(bf16[2,128,512]{2,1,0:T(8,128)(2,1)} %bitcast.8), channel_id=1, source_target_pairs={{0,2},{2,0},{1,3},{3,1},{4,6},{6,4},{5,7},{7,5},{8,10},{10,8},{9,1... | collective-permute-start | bytes 786440 | tf_op jit(solution)/shard_map/ppermute | solution.py:385
  21.4 10.0 %all-to-all-start.1 = ((f32[8,2,512]{2,1,0:T(2,128)}), f32[8,2,512]{2,1,0:T(2,128)S(1)}, u32[]{:S(2)}, u32[]{:S(2)}) async-start(f32[8,2,512]{2,1,0:T(2,128)} %get-tuple-element.30), calls=%async_computation.1 | async-start | bytes 65536 | tf_op jit(solution)/shard_map/all_to_all | solution.py:386

commit v3 on v2

--- a/solution.py
+++ b/solution.py
@@ -239,25 +239,23 @@
 
 
 def travel(queries, grads, keys, values, earlier, prefix):
-    steps, units, share, wide, narrow, lead, stats, stats_shape = specs_of(queries, keys, prefix)
-    rows = queries.shape[0]
+    groups = keys.shape[1] // HEAD_DIM
+    share = queries.shape[1] // HEAD_DIM // groups
     shifts = len(earlier) // 2
-    outs, out_specs = [], []
-    if shifts:
-        outs.append(jax.ShapeDtypeStruct((shifts, 2) + keys.shape, jnp.bfloat16))
-        out_specs.append(pl.BlockSpec((shifts, 2, rows, units * HEAD_DIM), lambda i: (0, 0, 0, i)))
-    outs += [jax.ShapeDtypeStruct(prefix.shape, jnp.float32), stats_shape]
-    out_specs += [lead, stats]
+    outs = [jax.ShapeDtypeStruct((shifts, 2) + keys.shape, jnp.bfloat16)] if shifts else []
+    outs.append(jax.ShapeDtypeStruct(prefix.shape, jnp.float32))
+    outs.append(specs_of(queries, keys, prefix)[-1])
+    arrays = [
+        pltpu.with_memory_space_constraint(x, pltpu.VMEM)
+        for x in (queries, grads, keys, values, *earlier, prefix)
+    ]
     result = pl.pallas_call(
         functools.partial(travel_kernel, shifts, share),
         out_shape=outs,
-        grid=(steps,),
-        in_specs=[wide, wide, narrow, narrow] + [narrow] * (2 * shifts) + [lead],
-        out_specs=out_specs,
-        compiler_params=pltpu.CompilerParams(
-            dimension_semantics=("arbitrary",), vmem_limit_bytes=VMEM_LIMIT
-        ),
-    )(queries, grads, keys, values, *earlier, prefix)
+        in_specs=[pl.BlockSpec(memory_space=pltpu.VMEM)] * len(arrays),
+        out_specs=[pl.BlockSpec(memory_space=pltpu.VMEM)] * len(outs),
+        compiler_params=pltpu.CompilerParams(vmem_limit_bytes=VMEM_LIMIT),
+    )(*arrays)
     return result if shifts else [None] + list(result)
 
 

time: 32.5 us -> 32.2 us (level)
  no operation moved by 1% of the time
where the time goes in v3:
time: 32.2 us; the launch traced here: 31.9 us
  starting transfers between devices  12.6 us (39%)
  Pallas kernels  11.4 us (35%)
  waiting for transfers between devices  5.35 us (17%)
  between operations  1.31 us (4%)
  local copies, waits for them, and re-layouts  1.22 us (4%)
    all_to_all x1, starting transfers between devices, shards(): lax.all_to_all(line, ('sample', 'fsdp'), split_axis=0, concat_axis=0, til...  5.65 us
    pallas_call x1, Pallas kernels, stay(): pl.pallas_call(functools.partial(stay_kernel, shifts, share), out_shape=[...  4.66 us
    all_to_all x1, waiting for transfers between devices, shards(): lax.all_to_all(line, ('sample', 'fsdp'), split_axis=0, concat_axis=0, til...  3.37 us
    all_to_all x1, starting transfers between devices, shards(): lax.all_to_all(dprefix, ('sample', 'fsdp'), split_axis=0, concat_axis=0,...  3.32 us
    pallas_call x1, Pallas kernels, travel(): pl.pallas_call(functools.partial(travel_kernel, shifts, share), out_shape...  3.24 us
    ppermute x1, starting transfers between devices, shards(): earlier.append(lax.ppermute(keys, 'fsdp', ring))  3.03 us
    pallas_call x1, Pallas kernels, prepare(): pl.pallas_call(functools.partial(prepare_kernel, comp_span), out_shape=[j...  2.65 us
    all_to_all x1, waiting for transfers between devices, shards(): lax.all_to_all(dprefix, ('sample', 'fsdp'), split_axis=0, concat_axis=0,...  1.97 us
  transfers between devices with their start and end apart: 5, of which 2 were waited for; matrix products, arithmetic and copies ran while one was open for 2% of the time, Pallas kernels for 23%

profile of v3, /device:TPU:0, one launch (start us, length us, event | category | flops | bytes accessed | tf_op | source)
XLA Modules:
  0.0 31.9 jit_solution(14566031428700569992)
XLA Ops:
  0.6 3.0 %collective-permute-start = (bf16[128,512]{1,0:T(8,128)(2,1)}, bf16[128,512]{1,0:T(8,128)(2,1)S(1)}, u32[]{:S(2)}, u32[]{:S(2)}) collective-permute-start(bf16[128,512]{1,0:T(8,128)(2,1)} %bitcast.15), channel_id=1, source_target_pairs={{0,2},{2,0},{1,3},{3,1},{4,6},{6,4},{5,7},{7,5},{8,10},{10,8},{9,1... | collective-permute-start | bytes 393224 | tf_op jit(solution)/shard_map/ppermute | solution.py:373
  3.7 0.0 copy-start.1
  3.7 0.0 copy-start
  3.7 0.1 collective-permute-start.1
  3.8 0.6 %copy-done.1 = bf16[1,1,512]{2,1,0:T(2,128)(2,1)S(1)} copy-done((bf16[1,1,512]{2,1,0:T(2,128)(2,1)S(1)}, bf16[1,1,512]{2,1,0:T(2,128)(2,1)}, u32[]{:S(2)}) %copy-start.1) | copy-done | bytes 1048
  4.3 0.0 copy-done
  4.4 0.6 %tile.2 = f32[8,2,512]{2,1,0:T(2,128)} broadcast(f32[2,512]{1,0:T(2,128)S(1)} %maximum_convert_fusion), dimensions={1,2} | broadcast | bytes 36864 | tf_op jit(solution)/shard_map/tile | solution.py:376
  5.0 5.7 %all-to-all-start = ((f32[8,2,512]{2,1,0:T(2,128)}), f32[8,2,512]{2,1,0:T(2,128)S(1)}, u32[]{:S(2)}, u32[]{:S(2)}) async-start(f32[8,2,512]{2,1,0:T(2,128)} %tile.2), calls=%async_computation | async-start | bytes 65536 | tf_op jit(solution)/shard_map/all_to_all | solution.py:377
  11.3 2.7 %shard_map.118 = (bf16[128,4096]{1,0:T(8,128)(2,1)S(1)}, bf16[128,4096]{1,0:T(8,128)(2,1)S(1)}, bf16[128,512]{1,0:T(8,128)(2,1)S(1)}, bf16[128,512]{1,0:T(8,128)(2,1)S(1)}) custom-call(s32[1,1]{1,0:T(1,128)S(6)} %copy.13.length_ref, bf16[128,4096]{1,0:T(8,128)(2,1)} %bitcast.13, bf16[128,4096]{1,0:T(8,128)(2,1)} %bitcast.14, bf16[128,512]{1,0:T(8,128)(2,1)} %bitcast.16, ...), custom_call_target="tpu_custom_call" | custom-call | flops 524288 | bytes 4718592 | tf_op jit(solution)/shard_map/pallas_call | solution.py:322
  14.0 3.4 %all-to-all-done.refs_2_ = f32[8,2,512]{2,1,0:T(2,128)S(1)} async-done(((f32[8,2,512]{2,1,0:T(2,128)}), f32[8,2,512]{2,1,0:T(2,128)S(1)}, u32[]{:S(2)}, u32[]{:S(2)}) %all-to-all-start) | async-done | bytes 32800 | tf_op jit(solution)/shard_map/all_to_all | solution.py:377
  17.3 0.0 collective-permute-done.refs_0_
  17.3 0.0 collective-permute-done.1.refs_1_
  17.3 3.2 %shard_map.119 = (bf16[1,2,128,512]{3,2,1,0:T(8,128)(2,1)}, f32[8,2,512]{2,1,0:T(2,128)}, f32[16,8,256]{2,1,0:T(8,128)}) custom-call(bf16[128,4096]{1,0:T(8,128)(2,1)S(1)} %get-tuple-element.21.q_ref, bf16[128,4096]{1,0:T(8,128)(2,1)S(1)} %get-tuple-element.22.g_ref, bf16[128,512]{1,0:T(8,128)(2,1)S(1)} %get-tuple-element.23.k_ref, ...), custom_call_target="tpu_custom_call" | custom-call | tf_op jit(solution)/shard_map/pallas_call | solution.py:252
  20.6 0.5 %collective-permute-start.2 = (bf16[2,128,512]{2,1,0:T(8,128)(2,1)}, bf16[2,128,512]{2,1,0:T(8,128)(2,1)S(1)}, u32[]{:S(2)}, u32[]{:S(2)}) collective-permute-start(bf16[2,128,512]{2,1,0:T(8,128)(2,1)} %bitcast.8), channel_id=1, source_target_pairs={{0,2},{2,0},{1,3},{3,1},{4,6},{6,4},{5,7},{7,5},{8,10},{10,8},{9,1... | collective-permute-start | bytes 786440 | tf_op jit(solution)/shard_map/ppermute | solution.py:383
  21.1 3.3 %all-to-all-start.1 = ((f32[8,2,512]{2,1,0:T(2,128)}), f32[8,2,512]{2,1,0:T(2,128)S(1)}, u32[]{:S(2)}, u32[]{:S(2)}) async-start(f32[8,2,512]{2,1,0:T(2,128)} %get-tuple-element.30), calls=%async_computation.1 | async-start | bytes 65536 | tf_op jit(solution)/shard_map/all_to_all | solution.py:384
  24.4 4.7 %shard_map.120 = (bf16[128,4096]{1,0:T(8,128)(2,1)}, bf16[128,4096]{1,0:T(8,128)(2,1)}, f32[128,512]{1,0:T(8,128)S(1)}, f32[128,512]{1,0:T(8,128)S(1)}) custom-call(bf16[128,4096]{1,0:T(8,128)(2,1)S(1)} %get-tuple-element.21.q_ref, bf16[128,4096]{1,0:T(8,128)(2,1)S(1)} %get-tuple-element.22.g_ref, bf16[128,512]{1,0:T(8,128)(2,1)S(1)} %get-tuple-element.23.k_ref, ...), custom_call_target="tpu_custom_call" | custom-call | flops 1384120320 | bytes 4194304 | tf_op jit(solution)/shard_map/pallas_call | solution.py:266
  29.0 2.0 %all-to-all-done.1.shares = f32[8,2,512]{2,1,0:T(2,128)S(1)} async-done(((f32[8,2,512]{2,1,0:T(2,128)}), f32[8,2,512]{2,1,0:T(2,128)S(1)}, u32[]{:S(2)}, u32[]{:S(2)}) %all-to-all-start.1) | async-done | bytes 32800 | tf_op jit(solution)/shard_map/all_to_all | solution.py:384
  31.0 0.0 collective-permute-done.2.refs_0_
  31.0 0.8 %shard_map.121 = (f32[128,512]{1,0:T(8,128)}, f32[128,512]{1,0:T(8,128)}, f32[1,512]{1,0:T(1,128)}, f32[1,512]{1,0:T(1,128)}) custom-call(f32[128,512]{1,0:T(8,128)S(1)} %get-tuple-element.28.dk, f32[128,512]{1,0:T(8,128)S(1)} %get-tuple-element.29.dv, f32[8,2,512]{2,1,0:T(2,128)S(1)} %all-to-all-done.1.shares, ...), custom_call_target="tpu_custom_call" | custom-call | tf_op jit(solution)/shard_map/pallas_call | solution.py:356
  (1 shorter events, 0.0 us)
Async XLA Ops:
  0.6 16.7 %collective-permute-start = (bf16[128,512]{1,0:T(8,128)(2,1)}, bf16[128,512]{1,0:T(8,128)(2,1)S(1)}, u32[]{:S(2)}, u32[]{:S(2)}) collective-permute-start(bf16[128,512]{1,0:T(8,128)(2,1)} %bitcast.15), channel_id=1, source_target_pairs={{0,2},{2,0},{1,3},{3,1},{4,6},{6,4},{5,7},{7,5},{8,10},{10,8},{9,1... | collective-permute-start | bytes 393224 | tf_op jit(solution)/shard_map/ppermute | solution.py:373
  3.7 0.7 %copy-start.1 = (bf16[1,1,512]{2,1,0:T(2,128)(2,1)S(1)}, bf16[1,1,512]{2,1,0:T(2,128)(2,1)}, u32[]{:S(2)}) copy-start(bf16[1,1,512]{2,1,0:T(2,128)(2,1)} %param.10) | copy-start | bytes 3076
  3.7 0.7 %copy-start = (bf16[1,1,512]{2,1,0:T(2,128)(2,1)S(1)}, bf16[1,1,512]{2,1,0:T(2,128)(2,1)}, u32[]{:S(2)}) copy-start(bf16[1,1,512]{2,1,0:T(2,128)(2,1)} %param.11) | copy-start | bytes 3076
  3.7 13.7 %collective-permute-start.1 = (bf16[128,512]{1,0:T(8,128)(2,1)}, bf16[128,512]{1,0:T(8,128)(2,1)S(1)}, u32[]{:S(2)}, u32[]{:S(2)}) collective-permute-start(bf16[128,512]{1,0:T(8,128)(2,1)} %bitcast.17), channel_id=1, source_target_pairs={{0,2},{2,0},{1,3},{3,1},{4,6},{6,4},{5,7},{7,5},{8,10},{10,8},{9,1... | collective-permute-start | bytes 393224 | tf_op jit(solution)/shard_map/ppermute | solution.py:374
  5.0 12.3 %all-to-all-start = ((f32[8,2,512]{2,1,0:T(2,128)}), f32[8,2,512]{2,1,0:T(2,128)S(1)}, u32[]{:S(2)}, u32[]{:S(2)}) async-start(f32[8,2,512]{2,1,0:T(2,128)} %tile.2), calls=%async_computation | async-start | bytes 65536 | tf_op jit(solution)/shard_map/all_to_all | solution.py:377
  20.6 10.4 %collective-permute-start.2 = (bf16[2,128,512]{2,1,0:T(8,128)(2,1)}, bf16[2,128,512]{2,1,0:T(8,128)(2,1)S(1)}, u32[]{:S(2)}, u32[]{:S(2)}) collective-permute-start(bf16[2,128,512]{2,1,0:T(8,128)(2,1)} %bitcast.8), channel_id=1, source_target_pairs={{0,2},{2,0},{1,3},{3,1},{4,6},{6,4},{5,7},{7,5},{8,10},{10,8},{9,1... | collective-permute-start | bytes 786440 | tf_op jit(solution)/shard_map/ppermute | solution.py:383
  21.1 10.0 %all-to-all-start.1 = ((f32[8,2,512]{2,1,0:T(2,128)}), f32[8,2,512]{2,1,0:T(2,128)S(1)}, u32[]{:S(2)}, u32[]{:S(2)}) async-start(f32[8,2,512]{2,1,0:T(2,128)} %get-tuple-element.30), calls=%async_computation.1 | async-start | bytes 65536 | tf_op jit(solution)/shard_map/all_to_all | solution.py:384

commit v4 on v3

--- a/solution.py
+++ b/solution.py
@@ -10,7 +10,7 @@
 HEAD_DIM = 128
 LOG2E = 1.4426950408889634
 UNITS = 2
-PARTS = 4
+PARTS = 2
 VMEM_LIMIT = 24 << 20
 
 NT = (((1,), (1,)), ((), ()))
@@ -169,6 +169,13 @@
 def stay_kernel(shifts, share, q_ref, g_ref, k_ref, v_ref, *refs):
     earlier, prefix, stats = refs[: 2 * shifts], refs[2 * shifts], refs[2 * shifts + 1]
     out, dq, dk, dv = refs[2 * shifts + 2 :]
+    span = dk.shape[1]
+    at = pl.multiple_of(pl.program_id(0) * span, span)
+    q_ref = q_ref.at[:, pl.ds(pl.multiple_of(at * share, span * share), span * share)]
+    g_ref = g_ref.at[:, pl.ds(pl.multiple_of(at * share, span * share), span * share)]
+    k_ref, v_ref = k_ref.at[:, pl.ds(at, span)], v_ref.at[:, pl.ds(at, span)]
+    earlier = [block.at[:, pl.ds(at, span)] for block in earlier]
+    prefix = prefix.at[:, :, pl.ds(at, span)]
     rows, prompt, padded, before, chunk, units = geometry(q_ref, prefix, k_ref, shifts, share)
     steps = rows // chunk
     scale = HEAD_DIM ** -0.5
@@ -260,7 +267,7 @@
 
 
 def stay(queries, grads, keys, values, earlier, prefix, marks):
-    steps, _, share, wide, narrow, lead, stats, _ = specs_of(queries, keys, prefix)
+    steps, _, share, wide, narrow, _, stats, _ = specs_of(queries, keys, prefix)
     shifts = len(earlier) // 2
     total = keys.shape[0] * (1 + shifts) + prefix.shape[0]
     return pl.pallas_call(
@@ -272,7 +279,7 @@
             jax.ShapeDtypeStruct(keys.shape, jnp.float32),
         ],
         grid=(steps,),
-        in_specs=[wide, wide, narrow, narrow] + [narrow] * (2 * shifts) + [lead, stats],
+        in_specs=[pl.BlockSpec(memory_space=pltpu.VMEM)] * (5 + 2 * shifts) + [stats],
         out_specs=[wide, wide, narrow, narrow],
         cost_estimate=pl.CostEstimate(
             flops=10 * queries.size * total,
@@ -280,10 +287,14 @@
             transcendentals=queries.size // HEAD_DIM * total,
         ),
         compiler_params=pltpu.CompilerParams(
-            dimension_semantics=("arbitrary",), vmem_limit_bytes=VMEM_LIMIT
+            dimension_semantics=("arbitrary",),
+            vmem_limit_bytes=VMEM_LIMIT,
         ),
     )(
-        queries, grads, keys, values, *earlier, prefix,
+        *(
+            pltpu.with_memory_space_constraint(x, pltpu.VMEM)
+            for x in (queries, grads, keys, values, *earlier, prefix)
+        ),
         pltpu.with_memory_space_constraint(marks, pltpu.HBM),
     )
 

time: 32.2 us -> 32.2 us (level)
  waiting for transfers between devices: 5.35 us -> 5.68 us
  transfers between devices with their start and end apart: 5 -> 5, of which waited for: 2 -> 2; matrix products, arithmetic and copies ran while one was open for 2% -> 2% of each run, Pallas kernels for 23% -> 22%
where the time goes in v4:
time: 32.2 us; the launch traced here: 31.9 us
  starting transfers between devices  12.6 us (39%)
  Pallas kernels  11.1 us (34%)
  waiting for transfers between devices  5.68 us (18%)
  between operations  1.31 us (4%)
  local copies, waits for them, and re-layouts  1.22 us (4%)
    all_to_all x1, starting transfers between devices, shards(): lax.all_to_all(line, ('sample', 'fsdp'), split_axis=0, concat_axis=0, til...  5.65 us
    pallas_call x1, Pallas kernels, stay(): pl.pallas_call(functools.partial(stay_kernel, shifts, share), out_shape=[...  4.55 us
    all_to_all x1, waiting for transfers between devices, shards(): lax.all_to_all(line, ('sample', 'fsdp'), split_axis=0, concat_axis=0, til...  3.6 us
    all_to_all x1, starting transfers between devices, shards(): lax.all_to_all(dprefix, ('sample', 'fsdp'), split_axis=0, concat_axis=0,...  3.32 us
    pallas_call x1, Pallas kernels, travel(): pl.pallas_call(functools.partial(travel_kernel, shifts, share), out_shape...  3.24 us
    ppermute x1, starting transfers between devices, shards(): earlier.append(lax.ppermute(keys, 'fsdp', ring))  3.03 us
    pallas_call x1, Pallas kernels, prepare(): pl.pallas_call(functools.partial(prepare_kernel, comp_span), out_shape=[j...  2.43 us
    all_to_all x1, waiting for transfers between devices, shards(): lax.all_to_all(dprefix, ('sample', 'fsdp'), split_axis=0, concat_axis=0,...  2.08 us
  transfers between devices with their start and end apart: 5, of which 2 were waited for; matrix products, arithmetic and copies ran while one was open for 2% of the time, Pallas kernels for 22%

profile of v4, /device:TPU:0, one launch (start us, length us, event | category | flops | bytes accessed | tf_op | source)
XLA Modules:
  0.0 31.9 jit_solution(12373163391492526405)
XLA Ops:
  0.6 3.0 %collective-permute-start = (bf16[128,512]{1,0:T(8,128)(2,1)}, bf16[128,512]{1,0:T(8,128)(2,1)S(1)}, u32[]{:S(2)}, u32[]{:S(2)}) collective-permute-start(bf16[128,512]{1,0:T(8,128)(2,1)} %bitcast.15), channel_id=1, source_target_pairs={{0,2},{2,0},{1,3},{3,1},{4,6},{6,4},{5,7},{7,5},{8,10},{10,8},{9,1... | collective-permute-start | bytes 393224 | tf_op jit(solution)/shard_map/ppermute | solution.py:384
  3.7 0.0 copy-start.1
  3.7 0.0 copy-start
  3.7 0.1 collective-permute-start.1
  3.8 0.6 %copy-done.1 = bf16[1,1,512]{2,1,0:T(2,128)(2,1)S(1)} copy-done((bf16[1,1,512]{2,1,0:T(2,128)(2,1)S(1)}, bf16[1,1,512]{2,1,0:T(2,128)(2,1)}, u32[]{:S(2)}) %copy-start.1) | copy-done | bytes 1048
  4.3 0.0 copy-done
  4.4 0.6 %tile.2 = f32[8,2,512]{2,1,0:T(2,128)} broadcast(f32[2,512]{1,0:T(2,128)S(1)} %maximum_convert_fusion), dimensions={1,2} | broadcast | bytes 36864 | tf_op jit(solution)/shard_map/tile | solution.py:387
  5.0 5.7 %all-to-all-start = ((f32[8,2,512]{2,1,0:T(2,128)}), f32[8,2,512]{2,1,0:T(2,128)S(1)}, u32[]{:S(2)}, u32[]{:S(2)}) async-start(f32[8,2,512]{2,1,0:T(2,128)} %tile.2), calls=%async_computation | async-start | bytes 65536 | tf_op jit(solution)/shard_map/all_to_all | solution.py:388
  11.3 2.4 %shard_map.118 = (bf16[128,4096]{1,0:T(8,128)(2,1)S(1)}, bf16[128,4096]{1,0:T(8,128)(2,1)S(1)}, bf16[128,512]{1,0:T(8,128)(2,1)S(1)}, bf16[128,512]{1,0:T(8,128)(2,1)S(1)}) custom-call(s32[1,1]{1,0:T(1,128)S(6)} %copy.13.length_ref, bf16[128,4096]{1,0:T(8,128)(2,1)} %bitcast.13, bf16[128,4096]{1,0:T(8,128)(2,1)} %bitcast.14, bf16[128,512]{1,0:T(8,128)(2,1)} %bitcast.16, ...), custom_call_target="tpu_custom_call" | custom-call | flops 524288 | bytes 4718592 | tf_op jit(solution)/shard_map/pallas_call | solution.py:333
  13.7 3.6 %all-to-all-done.refs_2_ = f32[8,2,512]{2,1,0:T(2,128)S(1)} async-done(((f32[8,2,512]{2,1,0:T(2,128)}), f32[8,2,512]{2,1,0:T(2,128)S(1)}, u32[]{:S(2)}, u32[]{:S(2)}) %all-to-all-start) | async-done | bytes 32800 | tf_op jit(solution)/shard_map/all_to_all | solution.py:388
  17.3 0.0 collective-permute-done.refs_0_
  17.3 0.0 collective-permute-done.1.refs_1_
  17.3 3.2 %shard_map.119 = (bf16[1,2,128,512]{3,2,1,0:T(8,128)(2,1)}, f32[8,2,512]{2,1,0:T(2,128)}, f32[16,8,256]{2,1,0:T(8,128)}) custom-call(bf16[128,4096]{1,0:T(8,128)(2,1)S(1)} %get-tuple-element.21.q_ref, bf16[128,4096]{1,0:T(8,128)(2,1)S(1)} %get-tuple-element.22.g_ref, bf16[128,512]{1,0:T(8,128)(2,1)S(1)} %get-tuple-element.23.k_ref, ...), custom_call_target="tpu_custom_call" | custom-call | tf_op jit(solution)/shard_map/pallas_call | solution.py:259
  20.6 0.5 %collective-permute-start.2 = (bf16[2,128,512]{2,1,0:T(8,128)(2,1)}, bf16[2,128,512]{2,1,0:T(8,128)(2,1)S(1)}, u32[]{:S(2)}, u32[]{:S(2)}) collective-permute-start(bf16[2,128,512]{2,1,0:T(8,128)(2,1)} %bitcast.8), channel_id=1, source_target_pairs={{0,2},{2,0},{1,3},{3,1},{4,6},{6,4},{5,7},{7,5},{8,10},{10,8},{9,1... | collective-permute-start | bytes 786440 | tf_op jit(solution)/shard_map/ppermute | solution.py:394
  21.1 3.3 %all-to-all-start.1 = ((f32[8,2,512]{2,1,0:T(2,128)}), f32[8,2,512]{2,1,0:T(2,128)S(1)}, u32[]{:S(2)}, u32[]{:S(2)}) async-start(f32[8,2,512]{2,1,0:T(2,128)} %get-tuple-element.30), calls=%async_computation.1 | async-start | bytes 65536 | tf_op jit(solution)/shard_map/all_to_all | solution.py:395
  24.4 4.5 %shard_map.120 = (bf16[128,4096]{1,0:T(8,128)(2,1)}, bf16[128,4096]{1,0:T(8,128)(2,1)}, f32[128,512]{1,0:T(8,128)S(1)}, f32[128,512]{1,0:T(8,128)S(1)}) custom-call(bf16[128,4096]{1,0:T(8,128)(2,1)S(1)} %get-tuple-element.21.q_ref, bf16[128,4096]{1,0:T(8,128)(2,1)S(1)} %get-tuple-element.22.g_ref, bf16[128,512]{1,0:T(8,128)(2,1)S(1)} %get-tuple-element.23.k_ref, ...), custom_call_target="tpu_custom_call" | custom-call | flops 1384120320 | bytes 4194304 | tf_op jit(solution)/shard_map/pallas_call | solution.py:273
  28.9 2.1 %all-to-all-done.1.shares = f32[8,2,512]{2,1,0:T(2,128)S(1)} async-done(((f32[8,2,512]{2,1,0:T(2,128)}), f32[8,2,512]{2,1,0:T(2,128)S(1)}, u32[]{:S(2)}, u32[]{:S(2)}) %all-to-all-start.1) | async-done | bytes 32800 | tf_op jit(solution)/shard_map/all_to_all | solution.py:395
  31.0 0.0 collective-permute-done.2.refs_0_
  31.0 0.8 %shard_map.121 = (f32[128,512]{1,0:T(8,128)}, f32[128,512]{1,0:T(8,128)}, f32[1,512]{1,0:T(1,128)}, f32[1,512]{1,0:T(1,128)}) custom-call(f32[128,512]{1,0:T(8,128)S(1)} %get-tuple-element.28.dk, f32[128,512]{1,0:T(8,128)S(1)} %get-tuple-element.29.dv, f32[8,2,512]{2,1,0:T(2,128)S(1)} %all-to-all-done.1.shares, ...), custom_call_target="tpu_custom_call" | custom-call | tf_op jit(solution)/shard_map/pallas_call | solution.py:367
  (1 shorter events, 0.0 us)
Async XLA Ops:
  0.6 16.7 %collective-permute-start = (bf16[128,512]{1,0:T(8,128)(2,1)}, bf16[128,512]{1,0:T(8,128)(2,1)S(1)}, u32[]{:S(2)}, u32[]{:S(2)}) collective-permute-start(bf16[128,512]{1,0:T(8,128)(2,1)} %bitcast.15), channel_id=1, source_target_pairs={{0,2},{2,0},{1,3},{3,1},{4,6},{6,4},{5,7},{7,5},{8,10},{10,8},{9,1... | collective-permute-start | bytes 393224 | tf_op jit(solution)/shard_map/ppermute | solution.py:384
  3.7 0.7 %copy-start.1 = (bf16[1,1,512]{2,1,0:T(2,128)(2,1)S(1)}, bf16[1,1,512]{2,1,0:T(2,128)(2,1)}, u32[]{:S(2)}) copy-start(bf16[1,1,512]{2,1,0:T(2,128)(2,1)} %param.10) | copy-start | bytes 3076
  3.7 0.7 %copy-start = (bf16[1,1,512]{2,1,0:T(2,128)(2,1)S(1)}, bf16[1,1,512]{2,1,0:T(2,128)(2,1)}, u32[]{:S(2)}) copy-start(bf16[1,1,512]{2,1,0:T(2,128)(2,1)} %param.11) | copy-start | bytes 3076
  3.7 13.7 %collective-permute-start.1 = (bf16[128,512]{1,0:T(8,128)(2,1)}, bf16[128,512]{1,0:T(8,128)(2,1)S(1)}, u32[]{:S(2)}, u32[]{:S(2)}) collective-permute-start(bf16[128,512]{1,0:T(8,128)(2,1)} %bitcast.17), channel_id=1, source_target_pairs={{0,2},{2,0},{1,3},{3,1},{4,6},{6,4},{5,7},{7,5},{8,10},{10,8},{9,1... | collective-permute-start | bytes 393224 | tf_op jit(solution)/shard_map/ppermute | solution.py:385
  5.0 12.3 %all-to-all-start = ((f32[8,2,512]{2,1,0:T(2,128)}), f32[8,2,512]{2,1,0:T(2,128)S(1)}, u32[]{:S(2)}, u32[]{:S(2)}) async-start(f32[8,2,512]{2,1,0:T(2,128)} %tile.2), calls=%async_computation | async-start | bytes 65536 | tf_op jit(solution)/shard_map/all_to_all | solution.py:388
  20.6 10.4 %collective-permute-start.2 = (bf16[2,128,512]{2,1,0:T(8,128)(2,1)}, bf16[2,128,512]{2,1,0:T(8,128)(2,1)S(1)}, u32[]{:S(2)}, u32[]{:S(2)}) collective-permute-start(bf16[2,128,512]{2,1,0:T(8,128)(2,1)} %bitcast.8), channel_id=1, source_target_pairs={{0,2},{2,0},{1,3},{3,1},{4,6},{6,4},{5,7},{7,5},{8,10},{10,8},{9,1... | collective-permute-start | bytes 786440 | tf_op jit(solution)/shard_map/ppermute | solution.py:394
  21.1 10.0 %all-to-all-start.1 = ((f32[8,2,512]{2,1,0:T(2,128)}), f32[8,2,512]{2,1,0:T(2,128)S(1)}, u32[]{:S(2)}, u32[]{:S(2)}) async-start(f32[8,2,512]{2,1,0:T(2,128)} %get-tuple-element.30), calls=%async_computation.1 | async-start | bytes 65536 | tf_op jit(solution)/shard_map/all_to_all | solution.py:395
